TPU v7x, 256 devices: a whole 4x4x8 slice. The times are simulated.
256 devices in a mesh: frac: 16 (over z, y_hi), rock: 16 (over y_lo, x, core).
Axes of the slice: x: 4, y: 4 (y_hi: 2, y_lo: 2; y = y_hi * 2 + y_lo), z: 8, core: 2. Of those that a mesh axis runs over, the one named last changes fastest.
Arguments:
- frac_conc: bfloat16 [512, 1024, 128], P(('frac', 'rock')), may hold values from -6 to 6
- frac_len: int32 [512], P(('frac', 'rock')), may hold values from 256 to 1024, as said below
- frac_flux: bfloat16 [512, 1024, 1024], P(('frac', 'rock')), may hold values from -0.1875 to 0.1875
- frac_inverse: bfloat16 [512, 1024, 1024], P(('frac', 'rock')), may hold values from -0.1875 to 0.1875
- inter_rows: int32 [16, 16, 16, 32], P('frac', 'rock'), may hold values from -1 to 2047, as said below
- wall_rows: int32 [16, 16, 16, 32], P('frac', 'rock'), may hold values from -1 to 2047, as said below
- wall_cells: int32 [16, 16, 16, 32], P('frac', 'rock'), may hold values from -1 to 2047, as said below
- rock_conc: float32 [128, 256, 2048], P(None, 'rock', 'frac'), may hold values from 0.05 to 4
- rock_diff: float32 [256, 2048], P('rock', 'frac'), may hold values from 0.5 to 1
- comp_rate: float32 [128], replicated, may hold values from 0.1 to 0.24
- cross_rate: float32 [128], replicated, may hold values from 0.1 to 0.8
- wall_rate: float32 [128], replicated, may hold values from 0.1 to 0.5
- sorb_cap: float32 [128], replicated, may hold values from 0.2 to 2
- sorb_aff: float32 [128], replicated, may hold values from 0.2 to 2
Outputs:
- frac_final: bfloat16 [512, 1024, 128], P(('frac', 'rock'))
- rock_final: float32 [128, 256, 2048], P(None, 'rock', 'frac')
Inputs may be any that keep to these rules, and one draw needn't show every extreme that they name: `frac_len`: one fracture has exactly 1024 live nodes. `inter_rows`: each entry is -1 or a live node row of device (f, r); entry [f, r, p, s] is live exactly when entry [p, r, f, s] is, and the two are one intersection; entries with p = f are -1; some device has 32 live entries towards some peer. `wall_rows`: each entry is -1 or a live node row of device (f, r); entry [f, r, q, s] is live exactly when wall_cells[f, q, r, s] is, and the two are one wall contact. `wall_cells`: each entry is -1 or a cell number of device (f, q)'s tile; for every f some q receives 32 live slots from every r; several slots may name one cell.
All inputs are finite; a program needn't handle non-finite values.
Results may differ from a plain program's by a relative error of at most 0.0064.
Values may be sent and summed in bfloat16 or wider, within the bound.
A program may use at most 64 MiB of HBM per device.

v0:
```python
import jax
import jax.numpy as jnp
from jax import lax
from jax.sharding import PartitionSpec as P

STEPS = 2


def with_halo(x, sides, width):
    for axis, dim in sides:
        count, length = (lax.axis_size(axis), x.shape[dim])
        up = [(i, (i + 1) % count) for i in range(count - 1)]
        down = [(j, i) for i, j in up]
        last = lax.slice_in_dim(x, length - width, length, axis=dim)
        initial = lax.slice_in_dim(x, 0, width, axis=dim)
        before = lax.ppermute(last, axis, up)
        after = lax.ppermute(initial, axis, down)
        x = jnp.concatenate([before, x, after], axis=dim)
    return x


def neighbour_sum(padded_field, padded_diff, centre_field, centre_diff):
    extent_x = centre_field.shape[1]
    extent_y = centre_field.shape[2]
    running = jnp.zeros_like(centre_field)
    for offset_x, offset_y in ((0, 1), (2, 1), (1, 0), (1, 2)):
        neighbour = padded_field[:, offset_x : offset_x + extent_x, offset_y : offset_y + extent_y]
        neighbour_diff = padded_diff[offset_x : offset_x + extent_x, offset_y : offset_y + extent_y]
        running = running + jnp.sqrt(centre_diff * neighbour_diff) * (neighbour - centre_field)
    return running


def retardation(field, sorb_cap, sorb_aff):
    return 1.0 + sorb_cap[:, None, None] / jnp.square(
        1.0 + sorb_aff[:, None, None] * jnp.abs(field)
    )


def local(
    frac_conc,
    frac_len,
    frac_flux,
    frac_inverse,
    inter_rows,
    wall_rows,
    wall_cells,
    rock_conc,
    rock_diff,
    comp_rate,
    cross_rate,
    wall_rate,
    sorb_cap,
    sorb_aff,
):
    frac_slots = frac_conc.shape[0]
    node_count = frac_conc.shape[1]
    components = frac_conc.shape[2]
    slot_rows = frac_slots * node_count
    tile_x = rock_conc.shape[1]
    tile_y = rock_conc.shape[2]
    tile_cells = tile_x * tile_y
    node_mask = (lax.broadcasted_iota(jnp.int32, (frac_slots, node_count), 1) < frac_len[:, None])[
        :, :, None
    ]
    zero_half = jnp.zeros((), jnp.bfloat16)
    concentration = jnp.where(node_mask, frac_conc, zero_half)
    pair_rows = inter_rows[0, 0]
    peers_frac = pair_rows.shape[0]
    capacity = pair_rows.shape[1]
    pair_live = (pair_rows >= 0).reshape(-1, 1)
    pair_clip = jnp.maximum(pair_rows, 0).reshape(-1)
    source_rows = wall_rows[0, 0]
    peers_rock = source_rows.shape[0]
    wall_slots = source_rows.shape[1]
    row_live = (source_rows >= 0).reshape(-1, 1)
    row_clip = jnp.maximum(source_rows, 0).reshape(-1)
    target_cells = wall_cells[0, 0]
    cell_live = (target_cells >= 0).reshape(-1, 1)
    cell_clip = jnp.maximum(target_cells, 0).reshape(-1)
    rock_field = rock_conc
    padded_diff = jnp.zeros((tile_x + 2, tile_y + 2), jnp.float32)
    for step_index in range(STEPS):
        flat_conc = concentration.reshape(slot_rows, components)
        own_values = jnp.where(pair_live, flat_conc[pair_clip], zero_half)
        remote_values = lax.all_to_all(
            own_values.reshape(peers_frac, capacity, components),
            "frac",
            split_axis=0,
            concat_axis=0,
            tiled=True,
        ).reshape(-1, components)
        cross_flux = jnp.where(
            pair_live,
            cross_rate * (remote_values.astype(jnp.float32) - own_values.astype(jnp.float32)),
            0.0,
        )
        inflow = jnp.zeros((slot_rows, components), jnp.float32).at[pair_clip].add(cross_flux)
        fracture_side = jnp.where(row_live, flat_conc[row_clip], zero_half)
        arrived = lax.all_to_all(
            fracture_side.reshape(peers_rock, wall_slots, components),
            "rock",
            split_axis=0,
            concat_axis=0,
            tiled=True,
        ).reshape(-1, components)
        rock_side = jnp.transpose(rock_field.reshape(components, tile_cells)[:, cell_clip]).astype(
            jnp.bfloat16
        )
        wall_flux = jnp.where(
            cell_live,
            wall_rate * (arrived.astype(jnp.float32) - rock_side.astype(jnp.float32)),
            0.0,
        )
        wall_gain = (
            jnp.zeros((components, tile_cells), jnp.float32)
            .at[:, cell_clip]
            .add(jnp.transpose(wall_flux))
            .reshape(components, tile_x, tile_y)
        )
        outflow = lax.all_to_all(
            wall_flux.reshape(peers_rock, wall_slots, components),
            "rock",
            split_axis=0,
            concat_axis=0,
            tiled=True,
        ).reshape(-1, components)
        inflow = inflow.at[row_clip].add(-outflow)
        if step_index == 0:
            stacked = jnp.concatenate([rock_field, rock_diff[None]], axis=0)
            padded = with_halo(stacked, (("frac", 2), ("rock", 1)), 1)
            padded_field = padded[:components]
            padded_diff = padded[components]
        else:
            padded_field = with_halo(
                rock_field.astype(jnp.bfloat16), (("frac", 2), ("rock", 1)), 1
            ).astype(rock_field.dtype)
        diffusion = comp_rate[:, None, None] * neighbour_sum(
            padded_field, padded_diff, rock_field, rock_diff
        )
        rock_field = rock_field + (diffusion + wall_gain) / retardation(
            rock_field, sorb_cap, sorb_aff
        )
        source = inflow.reshape(frac_slots, node_count, components)
        carried = jnp.einsum(
            "fij,fjc->fic", frac_flux, concentration, preferred_element_type=jnp.float32
        )
        mixed = (concentration.astype(jnp.float32) + carried + source).astype(jnp.bfloat16)
        solved = jnp.einsum("fij,fjc->fic", frac_inverse, mixed, preferred_element_type=jnp.float32)
        concentration = jnp.where(node_mask, solved, 0.0).astype(jnp.bfloat16)
    return (concentration, rock_field)


def solution(mesh):
    return jax.shard_map(
        local,
        mesh=mesh,
        in_specs=(
            P(("frac", "rock"), None, None),
            P(("frac", "rock")),
            P(("frac", "rock"), None, None),
            P(("frac", "rock"), None, None),
            P("frac", "rock", None, None),
            P("frac", "rock", None, None),
            P("frac", "rock", None, None),
            P(None, "rock", "frac"),
            P("rock", "frac"),
            P(),
            P(),
            P(),
            P(),
            P(),
        ),
        out_specs=(P(("frac", "rock"), None, None), P(None, "rock", "frac")),
        check_vma=False,
    )
```

profile of v0, /device:TPU:1, one launch (start us, length us, event | category | flops | bytes accessed | tf_op | source)
XLA Modules:
  0.0 186.6 jit_solution(12972551653448216430)
XLA Ops:
  8.1 7.1 %all-to-all-start.1 = ((bf16[16,32,128]{2,1,0:T(8,128)(2,1)}), bf16[16,32,128]{2,1,0:T(8,128)(2,1)}, u32[]{:S(2)}, u32[]{:S(2)}) async-start(bf16[16,32,128]{2,1,0:T(8,128)(2,1)} %broadcast_select_fusion.2), calls=%async_computation.1 | async-start | bytes 262144 | tf_op jit(solution)/shard_map/all_to_all | solution.py:99
  16.6 1.9 copy.93
  20.4 5.5 %collective-permute-start = (f32[129,16,1]{0,1,2:T(8,128)S(1)}, f32[129,16,1]{0,1,2:T(8,128)S(1)}, u32[]{:S(2)}, u32[]{:S(2)}) collective-permute-start(f32[129,16,1]{0,1,2:T(8,128)S(1)} %copy.92), channel_id=1, source_target_pairs={{0,16},{16,32},{32,48},{48,64},{64,80},{80,96},{96,112},{112,128},... | collective-permute-start | bytes 24776 | tf_op jit(solution)/shard_map/ppermute | solution.py:16
  34.7 2.7 %collective-permute-start.3 = (f32[129,1,130]{0,2,1:T(8,128)}, f32[129,1,130]{0,2,1:T(8,128)}, u32[]{:S(2)}, u32[]{:S(2)}) collective-permute-start(f32[129,1,130]{0,2,1:T(8,128)} %copy.97), channel_id=1, source_target_pairs={{1,0},{2,1},{3,2},{4,3},{5,4},{6,5},{7,6},{8,7},{9,8},{10,9},{11,1... | collective-permute-start | bytes 201248 | tf_op jit(solution)/shard_map/ppermute | solution.py:17
  37.5 3.3 %collective-permute-start.2 = (f32[129,1,130]{0,2,1:T(8,128)}, f32[129,1,130]{0,2,1:T(8,128)}, u32[]{:S(2)}, u32[]{:S(2)}) collective-permute-start(f32[129,1,130]{0,2,1:T(8,128)} %copy.96), channel_id=1, source_target_pairs={{0,1},{1,2},{2,3},{3,4},{4,5},{5,6},{6,7},{7,8},{8,9},{9,10},{10,1... | collective-permute-start | bytes 201248 | tf_op jit(solution)/shard_map/ppermute | solution.py:16
  40.8 2.8 %gather_fusion.2 = bf16[512,128]{1,0:T(8,128)(2,1)} fusion(bf16[128,2048]{0,1:T(8,128)(2,1)} %bitcast.82, s32[1024]{0:T(1024)S(1)} %pad_clamp_fusion), kind=kCustom, calls=%fused_computation.2 | custom fusion | bytes 264192 | tf_op jit(solution)/shard_map/gather | solution.py:106
  46.0 11.3 %all-to-all-start = ((bf16[16,32,128]{2,1,0:T(8,128)(2,1)}), bf16[16,32,128]{2,1,0:T(8,128)(2,1)}, u32[]{:S(2)}, u32[]{:S(2)}) async-start(bf16[16,32,128]{2,1,0:T(8,128)(2,1)} %broadcast_select_fusion.4), calls=%async_computation | async-start | bytes 262144 | tf_op jit(solution)/shard_map/all_to_all | solution.py:85
  57.3 1.8 fusion.49
  59.1 3.6 %scatter_custom_fusion.3 = f32[128,2048]{0,1:T(8,128)} fusion(s32[512]{0:T(512)} %copy-done.38, f32[512,128]{1,0:T(8,128)} %fusion.49, f32[]{:T(128)} %constant.5.clone.1), kind=kCustom, calls=%fused_computation.72 | custom fusion | flops 65536 | bytes 1049088 | tf_op jit(solution)/shard_map/scatter-add | solution.py:117
  62.7 2.6 %copy.104 = f32[128,16,128]{2,1,0:T(8,128)} copy(f32[128,16,128]{0,2,1:T(8,128)} %bitcast.85) | data formatting | bytes 2097152 | tf_op jit(solution)/shard_map/reshape | solution.py:118
  65.4 5.6 %fusion.71 = (bf16[128,16,128]{2,1,0:T(8,128)(2,1)S(1)}, f32[128,16,128]{2,1,0:T(8,128)}) fusion(f32[128,16,128]{2,1,0:T(8,128)S(1)} %copy-done, f32[128]{0:T(128)S(1)} %copy-done.41, f32[128]{0:T(128)S(1)} %copy-done.42, f32[128,16,128]{2,1,0:T(8,128)} %copy.104, f32[129,16,1]{2,1,0:T(8,128)S(1)} %copy.95, f32[1,16,128]{2,1,0:T(8,128)S(1)} %bitcast.97, ...), kind=kLoop, calls=%fused_computation.139 | loop fusion | flops 8912896 | bytes 3863184 | tf_op jit(solution)/shard_map/convert_element_type | solution.py:135
  72.9 5.8 %collective-permute-start.4 = (bf16[128,16,1]{2,1,0:T(8,128)(2,1)}, bf16[128,16,1]{2,1,0:T(8,128)(2,1)S(1)}, u32[]{:S(2)}, u32[]{:S(2)}) collective-permute-start(bf16[128,16,1]{2,1,0:T(8,128)(2,1)} %get-tuple-element.20), channel_id=1, source_target_pairs={{0,16},{16,32},{32,48},{48,64},{64,80},{80,96},{96,112},{112,128},... | collective-permute-start | bytes 12296 | tf_op jit(solution)/shard_map/ppermute | solution.py:16
  80.2 6.5 %all-to-all-start.2 = ((f32[16,32,128]{2,1,0:T(8,128)}), f32[16,32,128]{2,1,0:T(8,128)S(1)}, u32[]{:S(2)}, u32[]{:S(2)}) async-start(f32[16,32,128]{2,1,0:T(8,128)} %bitcast.90), calls=%async_computation.2 | async-start | bytes 524288 | tf_op jit(solution)/shard_map/all_to_all | solution.py:120
  87.3 2.1 %gather_fusion.5 = bf16[512,128]{1,0:T(8,128)(2,1)} fusion(bf16[128,2048]{0,1:T(8,128)(2,1)S(1)} %bitcast.83, s32[1024]{0:T(1024)} %copy-done.36), kind=kCustom, calls=%fused_computation.5 | custom fusion | bytes 264192 | tf_op jit(solution)/shard_map/gather | solution.py:106
  89.3 14.2 %collective-permute-done.4 = bf16[128,16,1]{2,1,0:T(8,128)(2,1)S(1)} collective-permute-done((bf16[128,16,1]{2,1,0:T(8,128)(2,1)}, bf16[128,16,1]{2,1,0:T(8,128)(2,1)S(1)}, u32[]{:S(2)}, u32[]{:S(2)}) %collective-permute-start.4) | collective-permute-done | bytes 4128 | tf_op jit(solution)/shard_map/ppermute | solution.py:16
  105.1 4.1 %collective-permute-start.6 = (bf16[128,1,130]{2,1,0:T(2,128)(2,1)}, bf16[128,1,130]{2,1,0:T(2,128)(2,1)}, u32[]{:S(2)}, u32[]{:S(2)}) collective-permute-start(bf16[128,1,130]{2,1,0:T(2,128)(2,1)} %get-tuple-element.16), channel_id=1, source_target_pairs={{0,1},{1,2},{2,3},{3,4},{4,5},{5,6},{6,7},{7,8},{8,9},{9,10},{10,1... | collective-permute-start | bytes 99848 | tf_op jit(solution)/shard_map/ppermute | solution.py:16
  109.2 1.9 %collective-permute-start.7 = (bf16[128,1,130]{2,1,0:T(2,128)(2,1)}, bf16[128,1,130]{2,1,0:T(2,128)(2,1)}, u32[]{:S(2)}, u32[]{:S(2)}) collective-permute-start(bf16[128,1,130]{2,1,0:T(2,128)(2,1)} %get-tuple-element.17), channel_id=1, source_target_pairs={{1,0},{2,1},{3,2},{4,3},{5,4},{6,5},{7,6},{8,7},{9,8},{10,9},{11,1... | collective-permute-start | bytes 99848 | tf_op jit(solution)/shard_map/ppermute | solution.py:17
  111.1 3.5 %scatter_custom_fusion = f32[2048,128]{1,0:T(8,128)S(1)} fusion(s32[512]{0:T(512)} %copy-done.37, f32[]{:T(128)} %constant.5.clone.1, bf16[512,128]{1,0:T(8,128)(2,1)} %bitcast.28, bf16[512,128]{1,0:T(8,128)(2,1)S(1)} %copy-done.11, f32[128]{0:T(128)} %param.24, pred[512]{0:T(512)(128)(4,1)S(1)} %ge.35, bf16[]{:T(256)} %constant.4.clone.1), kind=kCustom, calls=%fused_computation.76 | custom fusion | flops 458752 | bytes 1313280 | tf_op jit(solution)/shard_map/scatter-add | solution.py:97
  114.7 3.9 %scatter_fusion = f32[2048,128]{1,0:T(8,128)S(1)} fusion(f32[2048,128]{1,0:T(8,128)S(1)} %scatter_custom_fusion, s32[512]{0:T(512)S(1)} %copy-done.26, f32[512,128]{1,0:T(8,128)S(1)} %bitcast.89), kind=kCustom, calls=%fused_computation.7 | custom fusion | flops 65536 | bytes 788480 | tf_op jit(solution)/shard_map/scatter-add | solution.py:127
  119.0 6.4 %fusion.6 = bf16[2,128,1024]{2,1,0:T(8,128)(2,1)S(1)} fusion(bf16[2,1024,1024]{2,1,0:T(8,128)(2,1)} %param.17, f32[2,1024,128]{1,2,0:T(8,128)S(1)} %copy.90, bf16[2,1024,1024]{2,1,0:T(8,128)(2,1)} %param.16, pred[2,1024]{1,0:T(4,128)(4,1)S(1)} %copy-done.23, bf16[2,1024,128]{1,2,0:T(8,128)(2,1)S(1)} %copy-done.7), kind=kOutput, calls=%fused_computation.23 | convolution fusion | flops 1075838976 | bytes 10487808 | tf_op jit(solution)/shard_map/fij,fjc->fic/dot_general | solution.py:148
  129.2 4.9 %all-to-all-start.4 = ((bf16[16,32,128]{2,1,0:T(8,128)(2,1)}), bf16[16,32,128]{2,1,0:T(8,128)(2,1)S(1)}, u32[]{:S(2)}, u32[]{:S(2)}) async-start(bf16[16,32,128]{2,1,0:T(8,128)(2,1)} %broadcast_select_fusion.1), calls=%async_computation.4 | async-start | bytes 262144 | tf_op jit(solution)/shard_map/all_to_all | solution.py:99
  134.8 5.3 %all-to-all-done.4 = bf16[16,32,128]{2,1,0:T(8,128)(2,1)S(1)} async-done(((bf16[16,32,128]{2,1,0:T(8,128)(2,1)}), bf16[16,32,128]{2,1,0:T(8,128)(2,1)S(1)}, u32[]{:S(2)}, u32[]{:S(2)}) %all-to-all-start.4) | async-done | bytes 131104 | tf_op jit(solution)/shard_map/all_to_all | solution.py:99
  140.8 10.2 %all-to-all-start.3 = ((bf16[16,32,128]{2,1,0:T(8,128)(2,1)}), bf16[16,32,128]{2,1,0:T(8,128)(2,1)S(1)}, u32[]{:S(2)}, u32[]{:S(2)}) async-start(bf16[16,32,128]{2,1,0:T(8,128)(2,1)} %broadcast_select_fusion.3), calls=%async_computation.3 | async-start | bytes 262144 | tf_op jit(solution)/shard_map/all_to_all | solution.py:85
  151.0 3.1 %maximum_convert_fusion = f32[128,18,130]{2,1,0:T(8,128)S(1)} fusion(bf16[128,1,130]{2,1,0:T(2,128)(2,1)} %collective-permute-done.7, bf16[128,16,1]{2,1,0:T(8,128)(2,1)} %copy-done.9, bf16[128,16,128]{2,1,0:T(8,128)(2,1)} %copy-done.1, bf16[128,16,1]{2,1,0:T(8,128)(2,1)} %copy-done.8, bf16[128,1,130]{2,1,0:T(2,128)(2,1)} %collective-permute-done.6), kind=kLoop, calls=%fused_computation.12 | loop fusion | flops 2995200 | bytes 1797120 | tf_op jit(solution)/shard_map/convert_element_type | solution.py:136
  154.1 1.5 fusion.44
  155.6 3.6 %scatter_custom_fusion.5 = f32[128,2048]{0,1:T(8,128)} fusion(s32[512]{0:T(512)} %copy-done.38, f32[512,128]{1,0:T(8,128)} %fusion.44, f32[]{:T(128)} %constant.5.clone.1), kind=kCustom, calls=%fused_computation.70 | custom fusion | flops 65536 | bytes 1049088 | tf_op jit(solution)/shard_map/scatter-add | solution.py:117
  159.2 2.6 %copy.107 = f32[128,16,128]{2,1,0:T(8,128)} copy(f32[128,16,128]{0,2,1:T(8,128)} %bitcast.84) | data formatting | bytes 2097152 | tf_op jit(solution)/shard_map/reshape | solution.py:118
  162.5 5.0 %all-to-all-start.5 = ((f32[16,32,128]{2,1,0:T(8,128)}), f32[16,32,128]{2,1,0:T(8,128)S(1)}, u32[]{:S(2)}, u32[]{:S(2)}) async-start(f32[16,32,128]{2,1,0:T(8,128)} %bitcast.23), calls=%async_computation.5 | async-start | bytes 524288 | tf_op jit(solution)/shard_map/all_to_all | solution.py:120
  167.5 3.5 %fusion.14 = f32[128,16,128]{2,1,0:T(8,128)} fusion(f32[128,16,128]{2,1,0:T(8,128)} %get-tuple-element.13, f32[128,16,128]{2,1,0:T(8,128)} %copy.107, f32[128,18,130]{2,1,0:T(8,128)S(1)} %maximum_convert_fusion, f32[128]{0:T(128)} %param.27, f32[128]{0:T(128)} %param.26, f32[16,128]{1,0:T(8,128)} %copy-done.20, f32[16,128]{1,0:T(8,128)} %copy-done.21, ...), kind=kLoop, calls=%fused_computation.34 | loop fusion | flops 5505024 | bytes 7374336 | tf_op jit(solution)/shard_map/add | solution.py:140
  171.0 3.5 %scatter_custom_fusion.2 = f32[2048,128]{1,0:T(8,128)S(1)} fusion(s32[512]{0:T(512)} %copy-done.37, f32[]{:T(128)} %constant.5.clone.1, bf16[512,128]{1,0:T(8,128)(2,1)} %bitcast.91, bf16[512,128]{1,0:T(8,128)(2,1)S(1)} %gather_fusion.3, f32[128]{0:T(128)} %param.24, pred[512]{0:T(512)(128)(4,1)} %copy-done.39, bf16[]{:T(256)} %constant.4.clone.1), kind=kCustom, calls=%fused_computation.74 | custom fusion | flops 458752 | bytes 1313280 | tf_op jit(solution)/shard_map/scatter-add | solution.py:97
  174.8 4.0 %scatter_fusion.1 = f32[2048,128]{1,0:T(8,128)S(1)} fusion(f32[2048,128]{1,0:T(8,128)S(1)} %scatter_custom_fusion.2, s32[512]{0:T(512)} %copy-done.25, f32[512,128]{1,0:T(8,128)S(1)} %bitcast.88), kind=kCustom, calls=%fused_computation.10 | custom fusion | flops 65536 | bytes 788480 | tf_op jit(solution)/shard_map/scatter-add | solution.py:127
  179.2 6.4 %fusion.8 = bf16[2,1024,128]{1,2,0:T(8,128)(2,1)S(1)} fusion(bf16[2,1024,1024]{2,1,0:T(8,128)(2,1)} %param.17, f32[2,1024,128]{1,2,0:T(8,128)S(1)} %copy.106, bf16[2,128,1024]{2,1,0:T(8,128)(2,1)S(1)} %copy-done.5, bf16[2,1024,1024]{2,1,0:T(8,128)(2,1)} %param.16, pred[2,1024]{1,0:T(4,128)(4,1)S(1)} %copy-done.24), kind=kOutput, calls=%fused_computation.25 | convolution fusion | flops 1075314688 | bytes 10487808 | tf_op jit(solution)/shard_map/fij,fjc->fic/dot_general | solution.py:148
  (152 shorter events, 35.1 us)
Async XLA Ops:
  1.4 15.1 %copy-start.28 = (pred[16,32]{1,0:T(8,128)(4,1)}, pred[16,32]{1,0:T(8,128)(4,1)S(1)}, u32[]{:S(2)}) copy-start(pred[16,32]{1,0:T(8,128)(4,1)S(1)} %compare_bitcast_fusion) | copy-start | bytes 1540
  7.3 18.6 %copy-start.17 = (s32[1,1,16,32]{3,2,1,0:T(8,128)S(1)}, s32[1,1,16,32]{3,2,1,0:T(8,128)}, u32[]{:S(2)}) copy-start(s32[1,1,16,32]{3,2,1,0:T(8,128)} %param.18) | copy-start | bytes 6148
  7.3 18.6 %copy-start.27 = (s32[1,1,16,32]{3,2,1,0:T(8,128)S(1)}, s32[1,1,16,32]{3,2,1,0:T(8,128)}, u32[]{:S(2)}) copy-start(s32[1,1,16,32]{3,2,1,0:T(8,128)} %param.20) | copy-start | bytes 6148
  8.1 37.8 %all-to-all-start.1 = ((bf16[16,32,128]{2,1,0:T(8,128)(2,1)}), bf16[16,32,128]{2,1,0:T(8,128)(2,1)}, u32[]{:S(2)}, u32[]{:S(2)}) async-start(bf16[16,32,128]{2,1,0:T(8,128)(2,1)} %broadcast_select_fusion.2), calls=%async_computation.1 | async-start | bytes 262144 | tf_op jit(solution)/shard_map/all_to_all | solution.py:99
  18.4 13.0 %collective-permute-start.1 = (f32[129,16,1]{0,1,2:T(8,128)S(1)}, f32[129,16,1]{0,1,2:T(8,128)S(1)}, u32[]{:S(2)}, u32[]{:S(2)}) collective-permute-start(f32[129,16,1]{0,1,2:T(8,128)S(1)} %copy.93), channel_id=1, source_target_pairs={{16,0},{32,16},{48,32},{64,48},{80,64},{96,80},{112,96},{128,112},... | collective-permute-start | bytes 24776 | tf_op jit(solution)/shard_map/ppermute | solution.py:17
  20.4 10.3 %collective-permute-start = (f32[129,16,1]{0,1,2:T(8,128)S(1)}, f32[129,16,1]{0,1,2:T(8,128)S(1)}, u32[]{:S(2)}, u32[]{:S(2)}) collective-permute-start(f32[129,16,1]{0,1,2:T(8,128)S(1)} %copy.92), channel_id=1, source_target_pairs={{0,16},{16,32},{32,48},{48,64},{64,80},{80,96},{96,112},{112,128},... | collective-permute-start | bytes 24776 | tf_op jit(solution)/shard_map/ppermute | solution.py:16
  33.2 24.1 %copy-start.40 = (pred[512]{0:T(512)(128)(4,1)S(1)}, pred[512]{0:T(512)(128)(4,1)}, u32[]{:S(2)}) copy-start(pred[512]{0:T(512)(128)(4,1)} %ge.38) | copy-start | bytes 1540
  33.2 24.1 %copy-start.44 = (f32[128]{0:T(128)S(1)}, f32[128]{0:T(128)}, u32[]{:S(2)}) copy-start(f32[128]{0:T(128)} %param.25) | copy-start | bytes 1540
  34.7 8.8 %collective-permute-start.3 = (f32[129,1,130]{0,2,1:T(8,128)}, f32[129,1,130]{0,2,1:T(8,128)}, u32[]{:S(2)}, u32[]{:S(2)}) collective-permute-start(f32[129,1,130]{0,2,1:T(8,128)} %copy.97), channel_id=1, source_target_pairs={{1,0},{2,1},{3,2},{4,3},{5,4},{6,5},{7,6},{8,7},{9,8},{10,9},{11,1... | collective-permute-start | bytes 201248 | tf_op jit(solution)/shard_map/ppermute | solution.py:17
  37.5 7.2 %collective-permute-start.2 = (f32[129,1,130]{0,2,1:T(8,128)}, f32[129,1,130]{0,2,1:T(8,128)}, u32[]{:S(2)}, u32[]{:S(2)}) collective-permute-start(f32[129,1,130]{0,2,1:T(8,128)} %copy.96), channel_id=1, source_target_pairs={{0,1},{1,2},{2,3},{3,4},{4,5},{5,6},{6,7},{7,8},{8,9},{9,10},{10,1... | collective-permute-start | bytes 201248 | tf_op jit(solution)/shard_map/ppermute | solution.py:16
  45.7 19.7 %copy-start.41 = (f32[128]{0:T(128)S(1)}, f32[128]{0:T(128)}, u32[]{:S(2)}) copy-start(f32[128]{0:T(128)} %param.27) | copy-start | bytes 1540
  45.7 19.7 %copy-start.42 = (f32[128]{0:T(128)S(1)}, f32[128]{0:T(128)}, u32[]{:S(2)}) copy-start(f32[128]{0:T(128)} %param.26) | copy-start | bytes 1540
  45.7 19.6 %copy-start.43 = (f32[128]{0:T(128)S(1)}, f32[128]{0:T(128)}, u32[]{:S(2)}) copy-start(f32[128]{0:T(128)} %param.23) | copy-start | bytes 1540
  45.9 25.0 %copy-start.18 = (f32[16,128]{1,0:T(8,128)}, f32[16,128]{1,0:T(8,128)S(1)}, u32[]{:S(2)}) copy-start(f32[16,128]{1,0:T(8,128)S(1)} %get-tuple-element.23) | copy-start | bytes 24580
  45.9 25.0 %copy-start.20 = (f32[16,128]{1,0:T(8,128)}, f32[16,128]{1,0:T(8,128)S(1)}, u32[]{:S(2)}) copy-start(f32[16,128]{1,0:T(8,128)S(1)} %get-tuple-element.24) | copy-start | bytes 24580
  45.9 25.0 %copy-start.21 = (f32[16,128]{1,0:T(8,128)}, f32[16,128]{1,0:T(8,128)S(1)}, u32[]{:S(2)}) copy-start(f32[16,128]{1,0:T(8,128)S(1)} %get-tuple-element.25) | copy-start | bytes 24580
  46.0 34.2 %all-to-all-start = ((bf16[16,32,128]{2,1,0:T(8,128)(2,1)}), bf16[16,32,128]{2,1,0:T(8,128)(2,1)}, u32[]{:S(2)}, u32[]{:S(2)}) async-start(bf16[16,32,128]{2,1,0:T(8,128)(2,1)} %broadcast_select_fusion.4), calls=%async_computation | async-start | bytes 262144 | tf_op jit(solution)/shard_map/all_to_all | solution.py:85
  70.9 15.9 %copy-start.3 = (f32[128,16,128]{2,1,0:T(8,128)S(1)}, f32[128,16,128]{2,1,0:T(8,128)}, u32[]{:S(2)}) copy-start(f32[128,16,128]{2,1,0:T(8,128)} %get-tuple-element.13) | copy-start | bytes 3145732
  71.7 39.4 %copy-start.11 = (bf16[512,128]{1,0:T(8,128)(2,1)S(1)}, bf16[512,128]{1,0:T(8,128)(2,1)}, u32[]{:S(2)}) copy-start(bf16[512,128]{1,0:T(8,128)(2,1)} %copy-done.10) | copy-start | bytes 393220
  72.9 30.7 %copy-start.2 = (bf16[128,16,128]{2,1,0:T(8,128)(2,1)S(1)}, bf16[128,16,128]{2,1,0:T(8,128)(2,1)}, u32[]{:S(2)}) copy-start(bf16[128,16,128]{2,1,0:T(8,128)(2,1)} %copy-done.1) | copy-start | bytes 1572868
  72.9 30.7 %collective-permute-start.4 = (bf16[128,16,1]{2,1,0:T(8,128)(2,1)}, bf16[128,16,1]{2,1,0:T(8,128)(2,1)S(1)}, u32[]{:S(2)}, u32[]{:S(2)}) collective-permute-start(bf16[128,16,1]{2,1,0:T(8,128)(2,1)} %get-tuple-element.20), channel_id=1, source_target_pairs={{0,16},{16,32},{32,48},{48,64},{64,80},{80,96},{96,112},{112,128},... | collective-permute-start | bytes 12296 | tf_op jit(solution)/shard_map/ppermute | solution.py:16
  78.7 24.9 %collective-permute-start.5 = (bf16[128,16,1]{2,1,0:T(8,128)(2,1)}, bf16[128,16,1]{2,1,0:T(8,128)(2,1)S(1)}, u32[]{:S(2)}, u32[]{:S(2)}) collective-permute-start(bf16[128,16,1]{2,1,0:T(8,128)(2,1)} %get-tuple-element.21), channel_id=1, source_target_pairs={{16,0},{32,16},{48,32},{64,48},{80,64},{96,80},{112,96},{128,112},... | collective-permute-start | bytes 12296 | tf_op jit(solution)/shard_map/ppermute | solution.py:17
  80.2 34.4 %all-to-all-start.2 = ((f32[16,32,128]{2,1,0:T(8,128)}), f32[16,32,128]{2,1,0:T(8,128)S(1)}, u32[]{:S(2)}, u32[]{:S(2)}) async-start(f32[16,32,128]{2,1,0:T(8,128)} %bitcast.90), calls=%async_computation.2 | async-start | bytes 524288 | tf_op jit(solution)/shard_map/all_to_all | solution.py:120
  86.8 27.8 %copy-start.39 = (pred[512]{0:T(512)(128)(4,1)}, pred[512]{0:T(512)(128)(4,1)S(1)}, u32[]{:S(2)}) copy-start(pred[512]{0:T(512)(128)(4,1)S(1)} %ge.35) | copy-start | bytes 1540
  86.8 27.8 %copy-start.26 = (s32[512]{0:T(512)S(1)}, s32[512]{0:T(512)}, u32[]{:S(2)}) copy-start(s32[512]{0:T(512)} %copy-done.25) | copy-start | bytes 6148
  105.1 45.9 %collective-permute-start.6 = (bf16[128,1,130]{2,1,0:T(2,128)(2,1)}, bf16[128,1,130]{2,1,0:T(2,128)(2,1)}, u32[]{:S(2)}, u32[]{:S(2)}) collective-permute-start(bf16[128,1,130]{2,1,0:T(2,128)(2,1)} %get-tuple-element.16), channel_id=1, source_target_pairs={{0,1},{1,2},{2,3},{3,4},{4,5},{5,6},{6,7},{7,8},{8,9},{9,10},{10,1... | collective-permute-start | bytes 99848 | tf_op jit(solution)/shard_map/ppermute | solution.py:16
  109.2 41.8 %collective-permute-start.7 = (bf16[128,1,130]{2,1,0:T(2,128)(2,1)}, bf16[128,1,130]{2,1,0:T(2,128)(2,1)}, u32[]{:S(2)}, u32[]{:S(2)}) collective-permute-start(bf16[128,1,130]{2,1,0:T(2,128)(2,1)} %get-tuple-element.17), channel_id=1, source_target_pairs={{1,0},{2,1},{3,2},{4,3},{5,4},{6,5},{7,6},{8,7},{9,8},{10,9},{11,1... | collective-permute-start | bytes 99848 | tf_op jit(solution)/shard_map/ppermute | solution.py:17
  125.4 25.6 %copy-start.4 = (bf16[2,128,1024]{2,1,0:T(8,128)(2,1)}, bf16[2,128,1024]{2,1,0:T(8,128)(2,1)S(1)}, u32[]{:S(2)}) copy-start(bf16[2,128,1024]{2,1,0:T(8,128)(2,1)S(1)} %fusion.6) | copy-start | bytes 1572868
  128.4 25.7 %copy-start.13 = (bf16[512,128]{1,0:T(8,128)(2,1)S(1)}, bf16[512,128]{1,0:T(8,128)(2,1)}, u32[]{:S(2)}) copy-start(bf16[512,128]{1,0:T(8,128)(2,1)} %gather_fusion.5) | copy-start | bytes 393220
  129.2 10.9 %all-to-all-start.4 = ((bf16[16,32,128]{2,1,0:T(8,128)(2,1)}), bf16[16,32,128]{2,1,0:T(8,128)(2,1)S(1)}, u32[]{:S(2)}, u32[]{:S(2)}) async-start(bf16[16,32,128]{2,1,0:T(8,128)(2,1)} %broadcast_select_fusion.1), calls=%async_computation.4 | async-start | bytes 262144 | tf_op jit(solution)/shard_map/all_to_all | solution.py:99
  140.8 21.1 %all-to-all-start.3 = ((bf16[16,32,128]{2,1,0:T(8,128)(2,1)}), bf16[16,32,128]{2,1,0:T(8,128)(2,1)S(1)}, u32[]{:S(2)}, u32[]{:S(2)}) async-start(bf16[16,32,128]{2,1,0:T(8,128)(2,1)} %broadcast_select_fusion.3), calls=%async_computation.3 | async-start | bytes 262144 | tf_op jit(solution)/shard_map/all_to_all | solution.py:85
  162.5 12.3 %all-to-all-start.5 = ((f32[16,32,128]{2,1,0:T(8,128)}), f32[16,32,128]{2,1,0:T(8,128)S(1)}, u32[]{:S(2)}, u32[]{:S(2)}) async-start(f32[16,32,128]{2,1,0:T(8,128)} %bitcast.23), calls=%async_computation.5 | async-start | bytes 524288 | tf_op jit(solution)/shard_map/all_to_all | solution.py:120
  (27 other events, 172.6 us)
where the time goes:
time: 188 us; the launch traced here: 187 us
  starting transfers between devices  71.1 us (38%)
  other arithmetic  46.9 us (25%)
  local copies, waits for them, and re-layouts  34.5 us (18%)
  waiting for transfers between devices  19.8 us (11%)
  matrix products  12.7 us (7%)
    all_to_all x2, starting transfers between devices, local(): lax.all_to_all(own_values.reshape(peers_frac, capacity, components), 'fra...  21.5 us
    ppermute x4, starting transfers between devices, with_halo(): before = lax.ppermute(last, axis, up)  18.7 us
    ppermute x4, waiting for transfers between devices, with_halo(): before = lax.ppermute(last, axis, up)  14.2 us
    dot_general x2, matrix products, local(): jnp.einsum('fij,fjc->fic', frac_inverse, mixed, preferred_element_type=jn...  12.7 us
    all_to_all x2, starting transfers between devices, local(): lax.all_to_all(fracture_side.reshape(peers_rock, wall_slots, components),...  12 us
    all_to_all x2, starting transfers between devices, local(): lax.all_to_all(wall_flux.reshape(peers_rock, wall_slots, components), 'ro...  11.5 us
    scatter-add x2, other arithmetic, local(): inflow = inflow.at[row_clip].add(-outflow)  7.92 us
    unnamed x93, local copies, waits for them, and re-layouts  7.68 us
  transfers between devices with their start and end apart: 14, of which 3 were waited for; matrix products, arithmetic and copies ran while one was open for 39% of the time, Pallas kernels for 0%

commit v1 on v0

v1 whole, which is shorter than its diff:
```python
import functools

import jax
import jax.numpy as jnp
from jax import lax
from jax.experimental import pallas as pl
from jax.experimental.pallas import tpu as pltpu
from jax.sharding import PartitionSpec as P

STEPS = 2
N = 16
CAP = 32
C = 128
NODES = 1024
TX = 16
TY = 128
F32 = jnp.float32
BF16 = jnp.bfloat16
MESH = pl.DeviceIdType.MESH
BLK = 256


def rows(b, size):
    return pl.ds(pl.multiple_of(b * size, size), size)


def one_hot(hit):
    return jnp.where(hit, 1.0, 0.0).astype(BF16)


def decode(v):
    return jnp.where(v < 0, -1, v & (NODES - 1))


def kernel(
    conc_h,
    len_s,
    flux_h,
    inv_h,
    inter_v,
    wall_v,
    cells_v,
    rock_h,
    diff_v,
    comp_v,
    cross_v,
    wrate_v,
    cap_v,
    aff_v,
    conc_o,
    rock_o,
    conc_in,
    flux_v,
    inv_v,
    rock_in,
    conc2,
    mixed2,
    acc,
    table,
    idxb,
    rowb,
    g_op,
    gt_op,
    r_op,
    rt_op,
    f2,
    fr2,
    send_f,
    recv_f,
    send_r,
    recv_w,
    r_ref,
    rock2,
    s_bc,
    t_bc,
    w_ref,
    gain,
    dh,
    ye,
    yh,
    yeb,
    yhb,
    xeb,
    xhb,
    load_sem,
    x_send,
    x_recv,
    w_send,
    w_recv,
    v_send,
    v_recv,
    h_send,
    h_recv,
):
    me_f = lax.axis_index("frac")
    me_r = lax.axis_index("rock")

    loads = [
        pltpu.make_async_copy(src, dst, load_sem.at[i])
        for i, (src, dst) in enumerate(
            ((conc_h, conc_in), (rock_h, rock_in), (flux_h, flux_v), (inv_h, inv_v))
        )
    ]
    for load in loads:
        load.start()

    barrier = pltpu.get_barrier_semaphore()

    def greet(k, carry):
        pl.semaphore_signal(
            barrier, inc=1, device_id=(lax.rem(me_f + k, N), me_r), device_id_type=MESH
        )
        pl.semaphore_signal(
            barrier, inc=1, device_id=(me_f, lax.rem(me_r + k, N)), device_id_type=MESH
        )
        return carry

    lax.fori_loop(1, N, greet, 0)

    def x_copy(step, peer, slot):
        return pltpu.make_async_remote_copy(
            src_ref=send_f.at[step, peer],
            dst_ref=recv_f.at[step, slot],
            send_sem=x_send.at[step, peer],
            recv_sem=x_recv.at[step, slot],
            device_id=(peer, me_r),
            device_id_type=MESH,
        )

    def w_copy(step, peer, slot):
        return pltpu.make_async_remote_copy(
            src_ref=send_f.at[step, N + peer],
            dst_ref=recv_w.at[step, slot],
            send_sem=w_send.at[step, peer],
            recv_sem=w_recv.at[step, slot],
            device_id=(me_f, peer),
            device_id_type=MESH,
        )

    def v_copy(step, peer, slot):
        return pltpu.make_async_remote_copy(
            src_ref=send_r.at[step, peer],
            dst_ref=recv_f.at[step, N + slot],
            send_sem=v_send.at[step, peer],
            recv_sem=v_recv.at[step, slot],
            device_id=(me_f, peer),
            device_id_type=MESH,
        )

    def each_peer(me, act):
        def turn(k, carry):
            act(lax.rem(me + k, N))
            return carry

        lax.fori_loop(1, N, turn, 0)

    before_f = lax.rem(me_f + N - 1, N)
    after_f = lax.rem(me_f + 1, N)
    before_r = lax.rem(me_r + N - 1, N)
    after_r = lax.rem(me_r + 1, N)
    sides = (
        ((me_f, after_r), 0),
        ((me_f, before_r), 1),
        ((after_f, me_r), 2),
        ((before_f, me_r), 3),
    )

    def diff_copies():
        return [
            pltpu.make_async_remote_copy(
                src_ref=diff_v,
                dst_ref=dh.at[side],
                send_sem=h_send.at[0, side],
                recv_sem=h_recv.at[0, side],
                device_id=device,
                device_id_type=MESH,
            )
            for device, side in sides
        ]

    def halo_copies(step):
        out = []
        for device, side in sides:
            src, dst = (xeb, xhb) if side < 2 else (yeb, yhb)
            out.append(
                pltpu.make_async_remote_copy(
                    src_ref=src.at[step, side % 2],
                    dst_ref=dst.at[step, side % 2],
                    send_sem=h_send.at[1 + step, side],
                    recv_sem=h_recv.at[1 + step, side],
                    device_id=device,
                    device_id_type=MESH,
                )
            )
        return out

    table[...] = jnp.zeros_like(table)
    table[0:N, 0:CAP] = inter_v[...].astype(F32)
    table[N : 2 * N, 0:CAP] = wall_v[...].astype(F32)
    table[2 * N : 3 * N, 0:CAP] = cells_v[...].astype(F32)
    turned = jnp.transpose(table[...])
    for k in range(3 * N):
        idxb[k * CAP : (k + 1) * CAP, :] = jnp.broadcast_to(
            turned[0:CAP, k : k + 1], (CAP, C)
        ).astype(jnp.int32)

    lane = lax.broadcasted_iota(jnp.int32, (128, 128), 1)
    sub = lax.broadcasted_iota(jnp.int32, (128, 128), 0)

    def build_gather(op, first, count):
        def turn(b, carry):
            node = decode(idxb[rows(b + first, 128), :])
            for h in range(NODES // 128):
                op[rows(b, 128), h * 128 : (h + 1) * 128] = one_hot(node == lane + h * 128)
            return carry

        lax.fori_loop(0, count, turn, 0)

    def build_scatter(op, first, count):
        def turn(b, carry):
            for j in range(count):
                node = jnp.broadcast_to(
                    rowb[(first + j) * 8 : (first + j) * 8 + 1, :], (128, 128)
                )
                op[rows(b, 128), j * 128 : (j + 1) * 128] = one_hot(node == sub + b * 128)
            return carry

        lax.fori_loop(0, NODES // 128, turn, 0)

    build_gather(g_op, 0, 8)

    loads[0].wait()

    def mask_turn(b, carry):
        node = lax.broadcasted_iota(jnp.int32, (BLK, C), 0) + b * BLK
        for a in range(2):
            value = conc_in[a, rows(b, BLK), :].astype(F32)
            conc2[rows(b, BLK), a * C : (a + 1) * C] = jnp.where(
                node < len_s[a], value, 0.0
            ).astype(BF16)
        return carry

    lax.fori_loop(0, NODES // BLK, mask_turn, 0)

    def gather(op, source, first, dest, step, count):
        def turn(b, carry):
            found = jnp.dot(op[rows(b, BLK), :], source[...], preferred_element_type=F32)
            high = idxb[pl.ds(pl.multiple_of(first + b * BLK, 128), BLK), :] >= NODES
            own = jnp.where(high, found[:, C:], found[:, :C]).astype(BF16)
            dest[step, pl.ds(b * (BLK // CAP), BLK // CAP)] = own.reshape(BLK // CAP, CAP, C)
            return carry

        lax.fori_loop(0, count, turn, 0)

    def send_fractures(step):
        each_peer(me_f, lambda peer: x_copy(step, peer, me_f).start())
        each_peer(me_r, lambda peer: w_copy(step, peer, me_r).start())
        recv_f[step, me_f] = send_f[step, me_f]
        recv_w[step, me_r] = send_f[step, N + me_r]

    def send_rock(step):
        each_peer(me_r, lambda peer: v_copy(step, peer, me_r).start())
        for copy in halo_copies(step):
            copy.start()
        recv_f[step, N + me_r] = send_r[step, me_r]

    gather(g_op, conc2, 0, send_f, 0, 4)
    pl.semaphore_wait(barrier, 2 * (N - 1))
    for copy in diff_copies():
        copy.start()
    send_fractures(0)

    s_here = jnp.sqrt(diff_v[...])
    table[0:TX, :] = s_here
    turned = jnp.transpose(table[...])
    for x in range(TX):
        s_bc[x] = jnp.broadcast_to(turned[:, x : x + 1], (TY, C))

    def put_state(step, x, state):
        scaled = s_bc[x] * state
        r_ref[x] = state
        w_ref[step, x + 1, 8 : 8 + TY, :] = scaled
        ye[0, pl.ds(x, 1), :] = scaled[TY - 1 :, :]
        ye[1, pl.ds(x, 1), :] = scaled[:1, :]
        half = x // 8
        low = x % 8
        return half, low, state.astype(BF16)

    def edges(step):
        yeb[step] = ye[...].astype(BF16)
        xeb[step, 0] = w_ref[step, TX, 8 : 8 + TY, :].astype(BF16)
        xeb[step, 1] = w_ref[step, 1, 8 : 8 + TY, :].astype(BF16)

    loads[1].wait()
    for x in range(TX):
        half, low, small = put_state(0, x, jnp.transpose(rock_in[:, x, :]))
        rock2[low * TY : (low + 1) * TY, half * C : (half + 1) * C] = small
    edges(0)
    build_gather(r_op, 8, 4)
    gather(r_op, rock2, 2 * N * CAP, send_r, 0, 2)
    send_rock(0)

    for j in range(12):
        row = jnp.zeros((8, 128), F32)
        kind, first = divmod(4 * j, N)
        source = (inter_v, wall_v, cells_v)[kind]
        pieces = [source[first + i : first + i + 1, :] for i in range(4)]
        rowb[j * 8 : j * 8 + 1, :] = decode(jnp.concatenate(pieces, axis=1))
    build_scatter(gt_op, 0, 8)
    build_scatter(rt_op, 8, 4)

    def product():
        for a in range(2):

            def turn(b, carry):
                acc[a, rows(b, BLK), :] = conc2[rows(b, BLK), a * C : (a + 1) * C].astype(
                    F32
                ) + jnp.dot(
                    flux_v[a, rows(b, BLK), :],
                    conc2[:, a * C : (a + 1) * C],
                    preferred_element_type=F32,
                )
                return carry

            lax.fori_loop(0, NODES // BLK, turn, 0)

    loads[2].wait()
    product()

    for copy in diff_copies():
        copy.wait_recv()
    xrow = lax.broadcasted_iota(jnp.int32, (TX, TY), 0)
    ycol = lax.broadcasted_iota(jnp.int32, (TX, TY), 1)
    side_s = jnp.sqrt(dh[...])
    first_r, last_r = me_r == 0, me_r == N - 1
    first_f, last_f = me_f == 0, me_f == N - 1
    down_x = jnp.where(first_r, 0.0, side_s[0, TX - 1 :, :])
    up_x = jnp.where(last_r, 0.0, side_s[1, :1, :])
    down_y = jnp.where(first_f, 0.0, pltpu.roll(side_s[2], 1, 1))
    up_y = jnp.where(last_f, 0.0, pltpu.roll(side_s[3], TY - 1, 1))
    total = jnp.where(xrow == 0, down_x, pltpu.roll(s_here, 1, 0))
    total = total + jnp.where(xrow == TX - 1, up_x, pltpu.roll(s_here, TX - 1, 0))
    total = total + jnp.where(ycol == 0, down_y, pltpu.roll(s_here, 1, 1))
    total = total + jnp.where(ycol == TY - 1, up_y, pltpu.roll(s_here, TY - 1, 1))
    table[0:TX, :] = s_here * total
    turned = jnp.transpose(table[...])
    for x in range(TX):
        t_bc[x] = jnp.broadcast_to(turned[:, x : x + 1], (TY, C))

    cross_rate = cross_v[...]
    wall_rate = wrate_v[...]

    def flux_of(recv, send, dest, step, first, count):
        def turn(p, carry):
            rate = jnp.where(p < N, cross_rate, wall_rate) if first == 0 else wall_rate
            value = rate * (recv[step, p].astype(F32) - send[step, p].astype(F32))
            high = idxb[rows(first + p, CAP), :] >= NODES
            dest[rows(p, CAP), :C] = jnp.where(high, 0.0, value).astype(BF16)
            dest[rows(p, CAP), C:] = jnp.where(high, value, 0.0).astype(BF16)
            return carry

        lax.fori_loop(0, count, turn, 0)

    def solve(step):
        each_peer(me_f, lambda peer: x_copy(step, peer, peer).wait_recv())
        each_peer(me_r, lambda peer: v_copy(step, peer, peer).wait_recv())
        flux_of(recv_f, send_f, f2, step, 0, 2 * N)

        def mix(b, carry):
            inflow = jnp.dot(gt_op[rows(b, BLK), :], f2[...], preferred_element_type=F32)
            for a in range(2):
                mixed2[rows(b, BLK), a * C : (a + 1) * C] = (
                    acc[a, rows(b, BLK), :] + inflow[:, a * C : (a + 1) * C]
                ).astype(BF16)
            return carry

        lax.fori_loop(0, NODES // BLK, mix, 0)
        if step == 0:
            loads[3].wait()
        for a in range(2):

            def turn(b, carry):
                solved = jnp.dot(
                    inv_v[a, rows(b, BLK), :],
                    mixed2[:, a * C : (a + 1) * C],
                    preferred_element_type=F32,
                )
                node = lax.broadcasted_iota(jnp.int32, (BLK, C), 0) + b * BLK
                solved = jnp.where(node < len_s[a], solved, 0.0).astype(BF16)
                if step == STEPS - 1:
                    conc_o[a, rows(b, BLK), :] = solved
                else:
                    conc2[rows(b, BLK), a * C : (a + 1) * C] = solved
                return carry

            lax.fori_loop(0, NODES // BLK, turn, 0)

    comp_rate = comp_v[...]
    cap = cap_v[...]
    aff = aff_v[...]

    def diffuse(step):
        each_peer(me_r, lambda peer: w_copy(step, peer, peer).wait_recv())
        flux_of(recv_w, send_r, fr2, step, 2 * N, N)

        def spread(b, carry):
            gain[rows(b, BLK), :] = jnp.dot(
                rt_op[rows(b, BLK), :], fr2[...], preferred_element_type=F32
            )
            return carry

        lax.fori_loop(0, NODES // BLK, spread, 0)
        for copy in halo_copies(step):
            copy.wait_recv()
        w_ref[step, 0, 8 : 8 + TY, :] = jnp.where(first_r, 0.0, xhb[step, 0].astype(F32))
        w_ref[step, TX + 1, 8 : 8 + TY, :] = jnp.where(last_r, 0.0, xhb[step, 1].astype(F32))
        yh[0] = jnp.where(first_f, 0.0, yhb[step, 0].astype(F32))
        yh[1] = jnp.where(last_f, 0.0, yhb[step, 1].astype(F32))
        for x in range(TX):
            w_ref[step, x + 1, 7:8, :] = yh[0, x : x + 1, :]
            w_ref[step, x + 1, 8 + TY : 9 + TY, :] = yh[1, x : x + 1, :]
        for x in range(TX):
            half, low = divmod(x, 8)
            old = r_ref[x]
            around = (w_ref[step, x, 8 : 8 + TY, :] + w_ref[step, x + 2, 8 : 8 + TY, :]) + (
                w_ref[step, x + 1, 7 : 7 + TY, :] + w_ref[step, x + 1, 9 : 9 + TY, :]
            )
            diffusion = comp_rate * (s_bc[x] * around - t_bc[x] * old)
            added = diffusion + gain[low * TY : (low + 1) * TY, half * C : (half + 1) * C]
            root = 1.0 + aff * jnp.abs(old)
            square = root * root
            new = old + added * square / (square + cap)
            if step == STEPS - 1:
                rock_o[:, x, :] = jnp.transpose(new)
            else:
                _, _, small = put_state(step + 1, x, new)
                rock2[low * TY : (low + 1) * TY, half * C : (half + 1) * C] = small

    solve(0)
    gather(g_op, conc2, 0, send_f, 1, 4)
    send_fractures(1)
    diffuse(0)
    edges(1)
    gather(r_op, rock2, 2 * N * CAP, send_r, 1, 2)
    send_rock(1)
    product()
    diffuse(1)
    solve(1)

    for copy in diff_copies():
        copy.wait_send()
    for step in range(STEPS):
        each_peer(me_f, lambda peer: x_copy(step, peer, me_f).wait_send())
        each_peer(me_r, lambda peer: w_copy(step, peer, me_r).wait_send())
        each_peer(me_r, lambda peer: v_copy(step, peer, me_r).wait_send())
        for copy in halo_copies(step):
            copy.wait_send()


def local(
    frac_conc,
    frac_len,
    frac_flux,
    frac_inverse,
    inter_rows,
    wall_rows,
    wall_cells,
    rock_conc,
    rock_diff,
    comp_rate,
    cross_rate,
    wall_rate,
    sorb_cap,
    sorb_aff,
):
    any_spec = pl.BlockSpec(memory_space=pl.ANY)
    vmem = pl.BlockSpec(memory_space=pltpu.VMEM)
    smem = pl.BlockSpec(memory_space=pltpu.SMEM)
    dma = pltpu.SemaphoreType.DMA
    V = pltpu.VMEM
    return pl.pallas_call(
        kernel,
        out_shape=(
            jax.ShapeDtypeStruct(frac_conc.shape, BF16),
            jax.ShapeDtypeStruct(rock_conc.shape, F32),
        ),
        in_specs=[any_spec, smem, any_spec, any_spec, vmem, vmem, vmem, any_spec] + [vmem] * 6,
        out_specs=(vmem, vmem),
        scratch_shapes=[
            V((2, NODES, C), BF16),
            V((2, NODES, NODES), BF16),
            V((2, NODES, NODES), BF16),
            V((C, TX, TY), F32),
            V((NODES, 2 * C), BF16),
            V((NODES, 2 * C), BF16),
            V((2, NODES, C), F32),
            V((128, 128), F32),
            V((3 * N * CAP, C), jnp.int32),
            V((12 * 8, 128), jnp.int32),
            V((2 * N * CAP, NODES), BF16),
            V((NODES, 2 * N * CAP), BF16),
            V((N * CAP, NODES), BF16),
            V((NODES, N * CAP), BF16),
            V((2 * N * CAP, 2 * C), BF16),
            V((N * CAP, 2 * C), BF16),
            V((STEPS, 2 * N, CAP, C), BF16),
            V((STEPS, 2 * N, CAP, C), BF16),
            V((STEPS, N, CAP, C), BF16),
            V((STEPS, N, CAP, C), BF16),
            V((TX, TY, C), F32),
            V((NODES, 2 * C), BF16),
            V((TX, TY, C), F32),
            V((TX, TY, C), F32),
            V((STEPS, TX + 2, TY + 16, C), F32),
            V((NODES, 2 * C), F32),
            V((4, TX, TY), F32),
            V((2, TX, C), F32),
            V((2, TX, C), F32),
            V((STEPS, 2, TX, C), BF16),
            V((STEPS, 2, TX, C), BF16),
            V((STEPS, 2, TY, C), BF16),
            V((STEPS, 2, TY, C), BF16),
            dma((4,)),
            dma((STEPS, N)),
            dma((STEPS, N)),
            dma((STEPS, N)),
            dma((STEPS, N)),
            dma((STEPS, N)),
            dma((STEPS, N)),
            dma((STEPS + 1, 4)),
            dma((STEPS + 1, 4)),
        ],
        compiler_params=pltpu.CompilerParams(
            collective_id=0, has_side_effects=True, vmem_limit_bytes=56 << 20
        ),
        name="tracer_steps",
    )(
        frac_conc,
        frac_len,
        frac_flux,
        frac_inverse,
        inter_rows[0, 0],
        wall_rows[0, 0],
        wall_cells[0, 0],
        rock_conc,
        rock_diff,
        comp_rate.reshape(1, C),
        cross_rate.reshape(1, C),
        wall_rate.reshape(1, C),
        sorb_cap.reshape(1, C),
        sorb_aff.reshape(1, C),
    )


def solution(mesh):
    return jax.shard_map(
        local,
        mesh=mesh,
        in_specs=(
            P(("frac", "rock"), None, None),
            P(("frac", "rock")),
            P(("frac", "rock"), None, None),
            P(("frac", "rock"), None, None),
            P("frac", "rock", None, None),
            P("frac", "rock", None, None),
            P("frac", "rock", None, None),
            P(None, "rock", "frac"),
            P("rock", "frac"),
            P(),
            P(),
            P(),
            P(),
            P(),
        ),
        out_specs=(P(("frac", "rock"), None, None), P(None, "rock", "frac")),
        check_vma=False,
    )
```

time: 188 us -> 45.6 us (0.24)
  starting transfers between devices: 71.1 us -> 0 us
  other arithmetic: 46.9 us -> 0 us
  Pallas kernels: 0 us -> 40.6 us
  local copies, waits for them, and re-layouts: 34.5 us -> 4.13 us
  waiting for transfers between devices: 19.8 us -> 0 us
  matrix products: 12.7 us -> 0 us
    all_to_all x6 -> x0, starting transfers between devices: 45 us -> none  [the longest x2 21.5 us: local(): lax.all_to_all(own_values.reshape(peers_frac, capacity, components), 'fra...]
    pallas_call x0 -> x1, Pallas kernels: none -> 40.6 us  [local(): pl.pallas_call(kernel, out_shape=(jax.ShapeDtypeStruct(frac_conc.shape, B...]
    ppermute x8 -> x0, starting transfers between devices: 26.1 us -> none  [the longest x4 18.7 us: with_halo(): before = lax.ppermute(last, axis, up)]
    scatter-add x6 -> x0, other arithmetic: 22.1 us -> none  [the longest x2 7.92 us: local(): inflow = inflow.at[row_clip].add(-outflow)]
    ppermute x8 -> x0, waiting for transfers between devices: 14.3 us -> none  [the longest x4 14.2 us: with_halo(): before = lax.ppermute(last, axis, up)]
    dot_general x2 -> x0, matrix products: 12.7 us -> none  [local(): jnp.einsum('fij,fjc->fic', frac_inverse, mixed, preferred_element_type=jn...]
    gather x6 -> x0, local copies, waits for them, and re-layouts: 10.2 us -> none  [the longest x2 4.86 us: local(): rock_field.reshape(components, tile_cells)[:, cell_clip]]
    convert_element_type x2 -> x0, other arithmetic: 8.61 us -> none  [the longest x1 5.55 us: local(): rock_field.astype(jnp.bfloat16)]
  transfers between devices with their start and end apart: 14 -> 0, of which waited for: 3 -> 0; matrix products, arithmetic and copies ran while one was open for 39% -> 0% of each run, Pallas kernels for 0% -> 0%
where the time goes in v1:
time: 45.6 us; the launch traced here: 45.4 us
  Pallas kernels  40.6 us (89%)
  local copies, waits for them, and re-layouts  4.13 us (9%)
  between operations  0.64 us (1%)
    pallas_call x1, Pallas kernels, local(): pl.pallas_call(kernel, out_shape=(jax.ShapeDtypeStruct(frac_conc.shape, B...  40.6 us
    unnamed x2, local copies, waits for them, and re-layouts  4.13 us

profile of v1, /device:TPU:1, one launch (start us, length us, event | category | flops | bytes accessed | tf_op | source)
XLA Modules:
  0.0 45.4 jit_solution(10505183316468500098)
XLA Ops:
  0.6 40.6 %tracer_steps.1 = (bf16[2,1024,128]{2,1,0:T(8,128)(2,1)}, f32[128,16,128]{2,1,0:T(8,128)}) custom-call(bf16[2,1024,128]{2,1,0:T(8,128)(2,1)} %conc_h.1, s32[2]{0:T(128)} %len_s.1, bf16[2,1024,1024]{2,1,0:T(8,128)(2,1)} %flux_h.1, bf16[2,1024,1024]{2,1,0:T(8,128)(2,1)} %inv_h.1, s32[16,32]{1,0:T(8,128)} %bitcast.8, s32[16,32]{1,0:T(8,128)} %bitcast.9, ...), custom_call_target="tpu_custom_call" | custom-call | tf_op jit(solution)/shard_map/tracer_steps/pallas_call | solution.py:481
  41.3 1.9 %copy.18 = bf16[2,1024,128]{2,1,0:T(8,128)(2,1)} copy(bf16[2,1024,128]{2,1,0:T(8,128)(2,1)} %get-tuple-element.4) | data formatting | bytes 1048576
  43.1 2.3 %copy.19 = f32[128,16,128]{2,1,0:T(8,128)} copy(f32[128,16,128]{2,1,0:T(8,128)} %get-tuple-element.5) | data formatting | bytes 2097152

commit v2 on v1

--- a/solution.py
+++ b/solution.py
@@ -32,29 +32,44 @@
     return jnp.where(v < 0, -1, v & (NODES - 1))
 
 
+def solved_half(inv_v, mixed2, len_s, a):
+    solved = jnp.dot(inv_v[a], mixed2[:, a * C : (a + 1) * C], preferred_element_type=F32)
+    node = lax.broadcasted_iota(jnp.int32, solved.shape, 0)
+    return jnp.where(node < len_s[a], solved, 0.0).astype(BF16)
+
+
 def kernel(
     conc_h,
-    len_s,
+    len_h,
     flux_h,
     inv_h,
+    inter_h,
+    wall_h,
+    cells_h,
+    rock_h,
+    diff_h,
+    comp_h,
+    cross_h,
+    wrate_h,
+    cap_h,
+    aff_h,
+    inv_v,
+    mixed2,
+    rock_o,
+    len_s,
     inter_v,
     wall_v,
     cells_v,
-    rock_h,
     diff_v,
     comp_v,
     cross_v,
     wrate_v,
     cap_v,
     aff_v,
-    conc_o,
-    rock_o,
     conc_in,
     flux_v,
-    inv_v,
     rock_in,
     conc2,
-    mixed2,
     acc,
     table,
     idxb,
@@ -78,10 +93,8 @@
     dh,
     ye,
     yh,
-    yeb,
-    yhb,
-    xeb,
-    xhb,
+    edge_out,
+    edge_in,
     load_sem,
     x_send,
     x_recv,
@@ -91,6 +104,8 @@
     v_recv,
     h_send,
     h_recv,
+    d_send,
+    d_recv,
 ):
     me_f = lax.axis_index("frac")
     me_r = lax.axis_index("rock")
@@ -98,11 +113,26 @@
     loads = [
         pltpu.make_async_copy(src, dst, load_sem.at[i])
         for i, (src, dst) in enumerate(
-            ((conc_h, conc_in), (rock_h, rock_in), (flux_h, flux_v), (inv_h, inv_v))
+            (
+                (conc_h, conc_in),
+                (rock_h, rock_in),
+                (flux_h, flux_v),
+                (inv_h, inv_v),
+                (inter_h, inter_v),
+                (wall_h, wall_v),
+                (cells_h, cells_v),
+                (diff_h, diff_v),
+                (comp_h, comp_v),
+                (cross_h, cross_v),
+                (wrate_h, wrate_v),
+                (cap_h, cap_v),
+                (aff_h, aff_v),
+                (len_h, len_s),
+            )
         )
     ]
-    for load in loads:
-        load.start()
+    for i in (4, 5, 0, 13):
+        loads[i].start()
 
     barrier = pltpu.get_barrier_semaphore()
 
@@ -116,13 +146,15 @@
         return carry
 
     lax.fori_loop(1, N, greet, 0)
+    for i in (6, 7, 1, 2, 3, 8, 9, 10, 11, 12):
+        loads[i].start()
 
     def x_copy(step, peer, slot):
         return pltpu.make_async_remote_copy(
             src_ref=send_f.at[step, peer],
             dst_ref=recv_f.at[step, slot],
-            send_sem=x_send.at[step, peer],
-            recv_sem=x_recv.at[step, slot],
+            send_sem=x_send.at[step],
+            recv_sem=x_recv.at[step],
             device_id=(peer, me_r),
             device_id_type=MESH,
         )
@@ -131,8 +163,8 @@
         return pltpu.make_async_remote_copy(
             src_ref=send_f.at[step, N + peer],
             dst_ref=recv_w.at[step, slot],
-            send_sem=w_send.at[step, peer],
-            recv_sem=w_recv.at[step, slot],
+            send_sem=w_send.at[step],
+            recv_sem=w_recv.at[step],
             device_id=(me_f, peer),
             device_id_type=MESH,
         )
@@ -141,8 +173,8 @@
         return pltpu.make_async_remote_copy(
             src_ref=send_r.at[step, peer],
             dst_ref=recv_f.at[step, N + slot],
-            send_sem=v_send.at[step, peer],
-            recv_sem=v_recv.at[step, slot],
+            send_sem=v_send.at[step],
+            recv_sem=v_recv.at[step],
             device_id=(me_f, peer),
             device_id_type=MESH,
         )
@@ -170,8 +202,8 @@
             pltpu.make_async_remote_copy(
                 src_ref=diff_v,
                 dst_ref=dh.at[side],
-                send_sem=h_send.at[0, side],
-                recv_sem=h_recv.at[0, side],
+                send_sem=d_send,
+                recv_sem=d_recv,
                 device_id=device,
                 device_id_type=MESH,
             )
@@ -181,28 +213,39 @@
     def halo_copies(step):
         out = []
         for device, side in sides:
-            src, dst = (xeb, xhb) if side < 2 else (yeb, yhb)
+            part = (step, side % 2, pl.ds(0, TY) if side < 2 else pl.ds(TY, TX))
             out.append(
                 pltpu.make_async_remote_copy(
-                    src_ref=src.at[step, side % 2],
-                    dst_ref=dst.at[step, side % 2],
-                    send_sem=h_send.at[1 + step, side],
-                    recv_sem=h_recv.at[1 + step, side],
+                    src_ref=edge_out.at[part],
+                    dst_ref=edge_in.at[part],
+                    send_sem=h_send.at[step],
+                    recv_sem=h_recv.at[step],
                     device_id=device,
                     device_id_type=MESH,
                 )
             )
         return out
 
+    def drain(ref, sem):
+        pltpu.make_async_copy(ref, ref, sem).wait()
+
+    def peers_of(ref, step):
+        return ref.at[step, pl.ds(0, N - 1)]
+
     table[...] = jnp.zeros_like(table)
+    loads[4].wait()
+    loads[5].wait()
     table[0:N, 0:CAP] = inter_v[...].astype(F32)
     table[N : 2 * N, 0:CAP] = wall_v[...].astype(F32)
-    table[2 * N : 3 * N, 0:CAP] = cells_v[...].astype(F32)
-    turned = jnp.transpose(table[...])
-    for k in range(3 * N):
-        idxb[k * CAP : (k + 1) * CAP, :] = jnp.broadcast_to(
-            turned[0:CAP, k : k + 1], (CAP, C)
-        ).astype(jnp.int32)
+
+    def spread_slots(first, last):
+        turned = jnp.transpose(table[...])
+        for k in range(first, last):
+            idxb[k * CAP : (k + 1) * CAP, :] = jnp.broadcast_to(
+                turned[0:CAP, k : k + 1], (CAP, C)
+            ).astype(jnp.int32)
+
+    spread_slots(0, 2 * N)
 
     lane = lax.broadcasted_iota(jnp.int32, (128, 128), 1)
     sub = lax.broadcasted_iota(jnp.int32, (128, 128), 0)
@@ -230,6 +273,7 @@
     build_gather(g_op, 0, 8)
 
     loads[0].wait()
+    loads[13].wait()
 
     def mask_turn(b, carry):
         node = lax.broadcasted_iota(jnp.int32, (BLK, C), 0) + b * BLK
@@ -242,15 +286,12 @@
 
     lax.fori_loop(0, NODES // BLK, mask_turn, 0)
 
-    def gather(op, source, first, dest, step, count):
-        def turn(b, carry):
-            found = jnp.dot(op[rows(b, BLK), :], source[...], preferred_element_type=F32)
-            high = idxb[pl.ds(pl.multiple_of(first + b * BLK, 128), BLK), :] >= NODES
-            own = jnp.where(high, found[:, C:], found[:, :C]).astype(BF16)
-            dest[step, pl.ds(b * (BLK // CAP), BLK // CAP)] = own.reshape(BLK // CAP, CAP, C)
-            return carry
-
-        lax.fori_loop(0, count, turn, 0)
+    def gather(op, source, first, dest, step):
+        count = op.shape[0]
+        found = jnp.dot(op[...], source[...], preferred_element_type=F32)
+        high = idxb[first : first + count, :] >= NODES
+        own = jnp.where(high, found[:, C:], found[:, :C]).astype(BF16)
+        dest[step] = own.reshape(count // CAP, CAP, C)
 
     def send_fractures(step):
         each_peer(me_f, lambda peer: x_copy(step, peer, me_f).start())
@@ -264,11 +305,16 @@
             copy.start()
         recv_f[step, N + me_r] = send_r[step, me_r]
 
-    gather(g_op, conc2, 0, send_f, 0, 4)
+    gather(g_op, conc2, 0, send_f, 0)
+    loads[7].wait()
     pl.semaphore_wait(barrier, 2 * (N - 1))
+    send_fractures(0)
     for copy in diff_copies():
         copy.start()
-    send_fractures(0)
+
+    loads[6].wait()
+    table[2 * N : 3 * N, 0:CAP] = cells_v[...].astype(F32)
+    spread_slots(2 * N, 3 * N)
 
     s_here = jnp.sqrt(diff_v[...])
     table[0:TX, :] = s_here
@@ -287,9 +333,9 @@
         return half, low, state.astype(BF16)
 
     def edges(step):
-        yeb[step] = ye[...].astype(BF16)
-        xeb[step, 0] = w_ref[step, TX, 8 : 8 + TY, :].astype(BF16)
-        xeb[step, 1] = w_ref[step, 1, 8 : 8 + TY, :].astype(BF16)
+        edge_out[step, :, TY:, :] = ye[...].astype(BF16)
+        edge_out[step, 0, :TY, :] = w_ref[step, TX, 8 : 8 + TY, :].astype(BF16)
+        edge_out[step, 1, :TY, :] = w_ref[step, 1, 8 : 8 + TY, :].astype(BF16)
 
     loads[1].wait()
     for x in range(TX):
@@ -297,7 +343,7 @@
         rock2[low * TY : (low + 1) * TY, half * C : (half + 1) * C] = small
     edges(0)
     build_gather(r_op, 8, 4)
-    gather(r_op, rock2, 2 * N * CAP, send_r, 0, 2)
+    gather(r_op, rock2, 2 * N * CAP, send_r, 0)
     send_rock(0)
 
     for j in range(12):
@@ -311,24 +357,13 @@
 
     def product():
         for a in range(2):
-
-            def turn(b, carry):
-                acc[a, rows(b, BLK), :] = conc2[rows(b, BLK), a * C : (a + 1) * C].astype(
-                    F32
-                ) + jnp.dot(
-                    flux_v[a, rows(b, BLK), :],
-                    conc2[:, a * C : (a + 1) * C],
-                    preferred_element_type=F32,
-                )
-                return carry
-
-            lax.fori_loop(0, NODES // BLK, turn, 0)
+            conc = conc2[:, a * C : (a + 1) * C]
+            acc[a] = conc.astype(F32) + jnp.dot(flux_v[a], conc, preferred_element_type=F32)
 
     loads[2].wait()
     product()
 
-    for copy in diff_copies():
-        copy.wait_recv()
+    drain(dh, d_recv)
     xrow = lax.broadcasted_iota(jnp.int32, (TX, TY), 0)
     ycol = lax.broadcasted_iota(jnp.int32, (TX, TY), 1)
     side_s = jnp.sqrt(dh[...])
@@ -347,6 +382,8 @@
     for x in range(TX):
         t_bc[x] = jnp.broadcast_to(turned[:, x : x + 1], (TY, C))
 
+    for i in (8, 9, 10, 11, 12):
+        loads[i].wait()
     cross_rate = cross_v[...]
     wall_rate = wrate_v[...]
 
@@ -362,60 +399,34 @@
         lax.fori_loop(0, count, turn, 0)
 
     def solve(step):
-        each_peer(me_f, lambda peer: x_copy(step, peer, peer).wait_recv())
-        each_peer(me_r, lambda peer: v_copy(step, peer, peer).wait_recv())
+        drain(peers_of(recv_f, step), x_recv.at[step])
+        drain(peers_of(recv_f, step), v_recv.at[step])
         flux_of(recv_f, send_f, f2, step, 0, 2 * N)
 
-        def mix(b, carry):
-            inflow = jnp.dot(gt_op[rows(b, BLK), :], f2[...], preferred_element_type=F32)
-            for a in range(2):
-                mixed2[rows(b, BLK), a * C : (a + 1) * C] = (
-                    acc[a, rows(b, BLK), :] + inflow[:, a * C : (a + 1) * C]
-                ).astype(BF16)
-            return carry
-
-        lax.fori_loop(0, NODES // BLK, mix, 0)
-        if step == 0:
-            loads[3].wait()
+        inflow = jnp.dot(gt_op[...], f2[...], preferred_element_type=F32)
         for a in range(2):
-
-            def turn(b, carry):
-                solved = jnp.dot(
-                    inv_v[a, rows(b, BLK), :],
-                    mixed2[:, a * C : (a + 1) * C],
-                    preferred_element_type=F32,
-                )
-                node = lax.broadcasted_iota(jnp.int32, (BLK, C), 0) + b * BLK
-                solved = jnp.where(node < len_s[a], solved, 0.0).astype(BF16)
-                if step == STEPS - 1:
-                    conc_o[a, rows(b, BLK), :] = solved
-                else:
-                    conc2[rows(b, BLK), a * C : (a + 1) * C] = solved
-                return carry
-
-            lax.fori_loop(0, NODES // BLK, turn, 0)
+            mixed2[:, a * C : (a + 1) * C] = (
+                acc[a] + inflow[:, a * C : (a + 1) * C]
+            ).astype(BF16)
+
+    def advance():
+        loads[3].wait()
+        for a in range(2):
+            conc2[:, a * C : (a + 1) * C] = solved_half(inv_v, mixed2, len_s, a)
 
     comp_rate = comp_v[...]
     cap = cap_v[...]
     aff = aff_v[...]
 
     def diffuse(step):
-        each_peer(me_r, lambda peer: w_copy(step, peer, peer).wait_recv())
+        drain(peers_of(recv_w, step), w_recv.at[step])
         flux_of(recv_w, send_r, fr2, step, 2 * N, N)
-
-        def spread(b, carry):
-            gain[rows(b, BLK), :] = jnp.dot(
-                rt_op[rows(b, BLK), :], fr2[...], preferred_element_type=F32
-            )
-            return carry
-
-        lax.fori_loop(0, NODES // BLK, spread, 0)
-        for copy in halo_copies(step):
-            copy.wait_recv()
-        w_ref[step, 0, 8 : 8 + TY, :] = jnp.where(first_r, 0.0, xhb[step, 0].astype(F32))
-        w_ref[step, TX + 1, 8 : 8 + TY, :] = jnp.where(last_r, 0.0, xhb[step, 1].astype(F32))
-        yh[0] = jnp.where(first_f, 0.0, yhb[step, 0].astype(F32))
-        yh[1] = jnp.where(last_f, 0.0, yhb[step, 1].astype(F32))
+        gain[...] = jnp.dot(rt_op[...], fr2[...], preferred_element_type=F32)
+        drain(edge_in.at[step], h_recv.at[step])
+        w_ref[step, 0, 8 : 8 + TY, :] = jnp.where(first_r, 0.0, edge_in[step, 0, :TY, :].astype(F32))
+        w_ref[step, TX + 1, 8 : 8 + TY, :] = jnp.where(last_r, 0.0, edge_in[step, 1, :TY, :].astype(F32))
+        yh[0] = jnp.where(first_f, 0.0, edge_in[step, 0, TY:, :].astype(F32))
+        yh[1] = jnp.where(last_f, 0.0, edge_in[step, 1, TY:, :].astype(F32))
         for x in range(TX):
             w_ref[step, x + 1, 7:8, :] = yh[0, x : x + 1, :]
             w_ref[step, x + 1, 8 + TY : 9 + TY, :] = yh[1, x : x + 1, :]
@@ -437,24 +448,39 @@
                 rock2[low * TY : (low + 1) * TY, half * C : (half + 1) * C] = small
 
     solve(0)
-    gather(g_op, conc2, 0, send_f, 1, 4)
+    advance()
+    gather(g_op, conc2, 0, send_f, 1)
     send_fractures(1)
     diffuse(0)
     edges(1)
-    gather(r_op, rock2, 2 * N * CAP, send_r, 1, 2)
+    gather(r_op, rock2, 2 * N * CAP, send_r, 1)
     send_rock(1)
     product()
     diffuse(1)
     solve(1)
 
-    for copy in diff_copies():
-        copy.wait_send()
+    drain(dh, d_send)
     for step in range(STEPS):
-        each_peer(me_f, lambda peer: x_copy(step, peer, me_f).wait_send())
-        each_peer(me_r, lambda peer: w_copy(step, peer, me_r).wait_send())
-        each_peer(me_r, lambda peer: v_copy(step, peer, me_r).wait_send())
-        for copy in halo_copies(step):
-            copy.wait_send()
+        drain(peers_of(send_f, step), x_send.at[step])
+        drain(peers_of(send_f, step), w_send.at[step])
+        drain(peers_of(send_r, step), v_send.at[step])
+        drain(edge_out.at[step], h_send.at[step])
+
+
+def finish(len_h, inv_v, mixed2, rock_v, conc_h, rock_h, len_s, conc_v, sem):
+    rock_copy = pltpu.make_async_copy(rock_v, rock_h, sem.at[2])
+    rock_copy.start()
+    len_copy = pltpu.make_async_copy(len_h, len_s, sem.at[3])
+    len_copy.start()
+    len_copy.wait()
+    copies = []
+    for a in range(2):
+        conc_v[a] = solved_half(inv_v, mixed2, len_s, a)
+        copies.append(pltpu.make_async_copy(conc_v.at[a], conc_h.at[a], sem.at[a]))
+        copies[-1].start()
+    for copy in copies:
+        copy.wait()
+    rock_copy.wait()
 
 
 def local(
@@ -475,23 +501,34 @@
 ):
     any_spec = pl.BlockSpec(memory_space=pl.ANY)
     vmem = pl.BlockSpec(memory_space=pltpu.VMEM)
-    smem = pl.BlockSpec(memory_space=pltpu.SMEM)
     dma = pltpu.SemaphoreType.DMA
     V = pltpu.VMEM
-    return pl.pallas_call(
+    def stay(x):
+        return pltpu.with_memory_space_constraint(x, pltpu.HBM)
+
+    inverse, mixed, rock = pl.pallas_call(
         kernel,
         out_shape=(
-            jax.ShapeDtypeStruct(frac_conc.shape, BF16),
-            jax.ShapeDtypeStruct(rock_conc.shape, F32),
+            V(frac_inverse.shape, BF16),
+            V((NODES, 2 * C), BF16),
+            V(rock_conc.shape, F32),
         ),
-        in_specs=[any_spec, smem, any_spec, any_spec, vmem, vmem, vmem, any_spec] + [vmem] * 6,
-        out_specs=(vmem, vmem),
+        in_specs=[any_spec] * 14,
+        out_specs=(vmem, vmem, vmem),
         scratch_shapes=[
+            pltpu.SMEM((2,), jnp.int32),
+            V((N, CAP), jnp.int32),
+            V((N, CAP), jnp.int32),
+            V((N, CAP), jnp.int32),
+            V((TX, TY), F32),
+            V((1, C), F32),
+            V((1, C), F32),
+            V((1, C), F32),
+            V((1, C), F32),
+            V((1, C), F32),
             V((2, NODES, C), BF16),
             V((2, NODES, NODES), BF16),
-            V((2, NODES, NODES), BF16),
             V((C, TX, TY), F32),
-            V((NODES, 2 * C), BF16),
             V((NODES, 2 * C), BF16),
             V((2, NODES, C), F32),
             V((128, 128), F32),
@@ -516,40 +553,52 @@
             V((4, TX, TY), F32),
             V((2, TX, C), F32),
             V((2, TX, C), F32),
-            V((STEPS, 2, TX, C), BF16),
-            V((STEPS, 2, TX, C), BF16),
-            V((STEPS, 2, TY, C), BF16),
-            V((STEPS, 2, TY, C), BF16),
-            dma((4,)),
-            dma((STEPS, N)),
-            dma((STEPS, N)),
-            dma((STEPS, N)),
-            dma((STEPS, N)),
-            dma((STEPS, N)),
-            dma((STEPS, N)),
-            dma((STEPS + 1, 4)),
-            dma((STEPS + 1, 4)),
+            V((STEPS, 2, TY + TX, C), BF16),
+            V((STEPS, 2, TY + TX, C), BF16),
+            dma((14,)),
+            dma((STEPS,)),
+            dma((STEPS,)),
+            dma((STEPS,)),
+            dma((STEPS,)),
+            dma((STEPS,)),
+            dma((STEPS,)),
+            dma((STEPS,)),
+            dma((STEPS,)),
+            dma(()),
+            dma(()),
         ],
         compiler_params=pltpu.CompilerParams(
-            collective_id=0, has_side_effects=True, vmem_limit_bytes=56 << 20
+            collective_id=0, has_side_effects=True, vmem_limit_bytes=36 << 20
         ),
         name="tracer_steps",
     )(
-        frac_conc,
-        frac_len,
-        frac_flux,
-        frac_inverse,
-        inter_rows[0, 0],
-        wall_rows[0, 0],
-        wall_cells[0, 0],
-        rock_conc,
-        rock_diff,
-        comp_rate.reshape(1, C),
-        cross_rate.reshape(1, C),
-        wall_rate.reshape(1, C),
-        sorb_cap.reshape(1, C),
-        sorb_aff.reshape(1, C),
+        stay(frac_conc),
+        stay(frac_len),
+        stay(frac_flux),
+        stay(frac_inverse),
+        stay(inter_rows[0, 0]),
+        stay(wall_rows[0, 0]),
+        stay(wall_cells[0, 0]),
+        stay(rock_conc),
+        stay(rock_diff),
+        stay(comp_rate.reshape(1, C)),
+        stay(cross_rate.reshape(1, C)),
+        stay(wall_rate.reshape(1, C)),
+        stay(sorb_cap.reshape(1, C)),
+        stay(sorb_aff.reshape(1, C)),
     )
+    return pl.pallas_call(
+        finish,
+        out_shape=(
+            jax.ShapeDtypeStruct(frac_conc.shape, BF16),
+            jax.ShapeDtypeStruct(rock_conc.shape, F32),
+        ),
+        in_specs=[any_spec, vmem, vmem, vmem],
+        out_specs=(any_spec, any_spec),
+        scratch_shapes=[pltpu.SMEM((2,), jnp.int32), V(frac_conc.shape, BF16), dma((4,))],
+        compiler_params=pltpu.CompilerParams(vmem_limit_bytes=8 << 20),
+        name="finish",
+    )(stay(frac_len), inverse, mixed, rock)
 
 
 def solution(mesh):

time: 45.6 us -> 36.7 us (0.80)
  Pallas kernels: 40.6 us -> 35.9 us
  local copies, waits for them, and re-layouts: 4.13 us -> 0 us
    pallas_call x1 -> x2, Pallas kernels: 40.6 us -> 35.9 us  [the longest x1 33.2 us: local(): pl.pallas_call(kernel, out_shape=(V(frac_inverse.shape, BF16), V((NODES,...]
    unnamed x2 -> x0, local copies, waits for them, and re-layouts: 4.13 us -> none
where the time goes in v2:
time: 36.7 us; the launch traced here: 36.5 us
  Pallas kernels  35.9 us (98%)
  between operations  0.64 us (2%)
    pallas_call x1, Pallas kernels, local(): pl.pallas_call(kernel, out_shape=(V(frac_inverse.shape, BF16), V((NODES,...  33.2 us
    pallas_call x1, Pallas kernels, local(): pl.pallas_call(finish, out_shape=(jax.ShapeDtypeStruct(frac_conc.shape, B...  2.73 us

profile of v2, /device:TPU:1, one launch (start us, length us, event | category | flops | bytes accessed | tf_op | source)
XLA Modules:
  0.0 36.5 jit_solution(10498136935665626617)
XLA Ops:
  0.6 33.2 %tracer_steps.1 = (bf16[2,1024,1024]{2,1,0:T(8,128)(2,1)S(1)}, bf16[1024,256]{1,0:T(8,128)(2,1)S(1)}, f32[128,16,128]{2,1,0:T(8,128)S(1)}) custom-call(bf16[2,1024,128]{2,1,0:T(8,128)(2,1)} %conc_h.1, s32[2]{0:T(128)} %len_h.3, bf16[2,1024,1024]{2,1,0:T(8,128)(2,1)} %flux_h.1, bf16[2,1024,1024]{2,1,0:T(8,128)(2,1)} %inv_h.1, s32[16,32]{1,0:T(8,128)} %bitcast.8, ...), custom_call_target="tpu_custom_call" | custom-call | tf_op jit(solution)/shard_map/tracer_steps/pallas_call | solution.py:509
  33.8 2.7 %finish.1 = (bf16[2,1024,128]{2,1,0:T(8,128)(2,1)}, f32[128,16,128]{2,1,0:T(8,128)}) custom-call(s32[2]{0:T(128)} %len_h.3, bf16[2,1024,1024]{2,1,0:T(8,128)(2,1)S(1)} %get-tuple-element.5.inv_v, bf16[1024,256]{1,0:T(8,128)(2,1)S(1)} %get-tuple-element.6.mixed2, f32[128,16,128]{2,1,0:T(8,128)S(1)} %get-tuple-element.7.rock_v), custom_call_target="tpu_custom_call" | custom-call | tf_op jit(solution)/shard_map/finish/pallas_call | solution.py:590

commit v3 on v2

--- a/solution.py
+++ b/solution.py
@@ -32,10 +32,17 @@
     return jnp.where(v < 0, -1, v & (NODES - 1))
 
 
-def solved_half(inv_v, mixed2, len_s, a):
-    solved = jnp.dot(inv_v[a], mixed2[:, a * C : (a + 1) * C], preferred_element_type=F32)
-    node = lax.broadcasted_iota(jnp.int32, solved.shape, 0)
-    return jnp.where(node < len_s[a], solved, 0.0).astype(BF16)
+FAR_FIRST = sorted(range(1, N), key=lambda k: abs(k - N // 2))
+
+
+def solved_rows(inv_v, mixed2, lens, a, first, count):
+    solved = jnp.dot(
+        inv_v[a, first : first + count, :],
+        mixed2[:, a * C : (a + 1) * C],
+        preferred_element_type=F32,
+    )
+    node = lax.broadcasted_iota(jnp.int32, (count, C), 0) + first
+    return jnp.where(node < lens[a : a + 1, :], solved, 0.0).astype(BF16)
 
 
 def kernel(
@@ -56,6 +63,7 @@
     inv_v,
     mixed2,
     rock_o,
+    lens,
     len_s,
     inter_v,
     wall_v,
@@ -89,7 +97,7 @@
     s_bc,
     t_bc,
     w_ref,
-    gain,
+    fac,
     dh,
     ye,
     yh,
@@ -131,22 +139,19 @@
             )
         )
     ]
-    for i in (4, 5, 0, 13):
-        loads[i].start()
-
     barrier = pltpu.get_barrier_semaphore()
 
-    def greet(k, carry):
+    loads[4].start()
+    loads[5].start()
+    for k in FAR_FIRST:
         pl.semaphore_signal(
             barrier, inc=1, device_id=(lax.rem(me_f + k, N), me_r), device_id_type=MESH
         )
+    for k in FAR_FIRST:
         pl.semaphore_signal(
             barrier, inc=1, device_id=(me_f, lax.rem(me_r + k, N)), device_id_type=MESH
         )
-        return carry
-
-    lax.fori_loop(1, N, greet, 0)
-    for i in (6, 7, 1, 2, 3, 8, 9, 10, 11, 12):
+    for i in (0, 13, 7, 1, 6, 2, 3, 8, 9, 10, 11, 12):
         loads[i].start()
 
     def x_copy(step, peer, slot):
@@ -180,11 +185,8 @@
         )
 
     def each_peer(me, act):
-        def turn(k, carry):
+        for k in FAR_FIRST:
             act(lax.rem(me + k, N))
-            return carry
-
-        lax.fori_loop(1, N, turn, 0)
 
     before_f = lax.rem(me_f + N - 1, N)
     after_f = lax.rem(me_f + 1, N)
@@ -274,6 +276,8 @@
 
     loads[0].wait()
     loads[13].wait()
+    for a in range(2):
+        lens[a : a + 1, :] = jnp.full((1, C), len_s[a], jnp.int32)
 
     def mask_turn(b, carry):
         node = lax.broadcasted_iota(jnp.int32, (BLK, C), 0) + b * BLK
@@ -286,35 +290,28 @@
 
     lax.fori_loop(0, NODES // BLK, mask_turn, 0)
 
-    def gather(op, source, first, dest, step):
-        count = op.shape[0]
-        found = jnp.dot(op[...], source[...], preferred_element_type=F32)
-        high = idxb[first : first + count, :] >= NODES
-        own = jnp.where(high, found[:, C:], found[:, :C]).astype(BF16)
-        dest[step] = own.reshape(count // CAP, CAP, C)
-
-    def send_fractures(step):
+    def gather(op, source, first, dest, step, part):
+        for begin in range(part * N * CAP, (part + 1) * N * CAP, BLK):
+            found = jnp.dot(op[begin : begin + BLK, :], source[...], preferred_element_type=F32)
+            high = idxb[first + begin : first + begin + BLK, :] >= NODES
+            own = jnp.where(high, found[:, C:], found[:, :C]).astype(BF16)
+            dest[step, begin // CAP : (begin + BLK) // CAP] = own.reshape(BLK // CAP, CAP, C)
+
+    def send_crossing(step):
         each_peer(me_f, lambda peer: x_copy(step, peer, me_f).start())
+        recv_f[step, me_f] = send_f[step, me_f]
+
+    def send_walls(step):
         each_peer(me_r, lambda peer: w_copy(step, peer, me_r).start())
-        recv_f[step, me_f] = send_f[step, me_f]
         recv_w[step, me_r] = send_f[step, N + me_r]
 
     def send_rock(step):
         each_peer(me_r, lambda peer: v_copy(step, peer, me_r).start())
-        for copy in halo_copies(step):
-            copy.start()
         recv_f[step, N + me_r] = send_r[step, me_r]
 
-    gather(g_op, conc2, 0, send_f, 0)
+    gather(g_op, conc2, 0, send_f, 0, 0)
+    gather(g_op, conc2, 0, send_f, 0, 1)
     loads[7].wait()
-    pl.semaphore_wait(barrier, 2 * (N - 1))
-    send_fractures(0)
-    for copy in diff_copies():
-        copy.start()
-
-    loads[6].wait()
-    table[2 * N : 3 * N, 0:CAP] = cells_v[...].astype(F32)
-    spread_slots(2 * N, 3 * N)
 
     s_here = jnp.sqrt(diff_v[...])
     table[0:TX, :] = s_here
@@ -328,9 +325,8 @@
         w_ref[step, x + 1, 8 : 8 + TY, :] = scaled
         ye[0, pl.ds(x, 1), :] = scaled[TY - 1 :, :]
         ye[1, pl.ds(x, 1), :] = scaled[:1, :]
-        half = x // 8
-        low = x % 8
-        return half, low, state.astype(BF16)
+        half, low = divmod(x, 8)
+        rock2[low * TY : (low + 1) * TY, half * C : (half + 1) * C] = state.astype(BF16)
 
     def edges(step):
         edge_out[step, :, TY:, :] = ye[...].astype(BF16)
@@ -339,11 +335,19 @@
 
     loads[1].wait()
     for x in range(TX):
-        half, low, small = put_state(0, x, jnp.transpose(rock_in[:, x, :]))
-        rock2[low * TY : (low + 1) * TY, half * C : (half + 1) * C] = small
+        put_state(0, x, jnp.transpose(rock_in[:, x, :]))
     edges(0)
+
+    pl.semaphore_wait(barrier, 2 * (N - 1))
+    for copy in diff_copies() + halo_copies(0):
+        copy.start()
+    send_crossing(0)
+    send_walls(0)
+    loads[6].wait()
+    table[2 * N : 3 * N, 0:CAP] = cells_v[...].astype(F32)
+    spread_slots(2 * N, 3 * N)
     build_gather(r_op, 8, 4)
-    gather(r_op, rock2, 2 * N * CAP, send_r, 0)
+    gather(r_op, rock2, 2 * N * CAP, send_r, 0, 0)
     send_rock(0)
 
     for j in range(12):
@@ -352,13 +356,17 @@
         source = (inter_v, wall_v, cells_v)[kind]
         pieces = [source[first + i : first + i + 1, :] for i in range(4)]
         rowb[j * 8 : j * 8 + 1, :] = decode(jnp.concatenate(pieces, axis=1))
+    build_scatter(rt_op, 8, 4)
     build_scatter(gt_op, 0, 8)
-    build_scatter(rt_op, 8, 4)
 
     def product():
         for a in range(2):
             conc = conc2[:, a * C : (a + 1) * C]
-            acc[a] = conc.astype(F32) + jnp.dot(flux_v[a], conc, preferred_element_type=F32)
+            for first in range(0, NODES, BLK):
+                part = slice(first, first + BLK)
+                acc[a, part, :] = conc[part, :].astype(F32) + jnp.dot(
+                    flux_v[a, part, :], conc, preferred_element_type=F32
+                )
 
     loads[2].wait()
     product()
@@ -387,41 +395,51 @@
     cross_rate = cross_v[...]
     wall_rate = wrate_v[...]
 
-    def flux_of(recv, send, dest, step, first, count):
+    def flux_of(rate, recv, send, dest, step, first, begin):
         def turn(p, carry):
-            rate = jnp.where(p < N, cross_rate, wall_rate) if first == 0 else wall_rate
             value = rate * (recv[step, p].astype(F32) - send[step, p].astype(F32))
             high = idxb[rows(first + p, CAP), :] >= NODES
             dest[rows(p, CAP), :C] = jnp.where(high, 0.0, value).astype(BF16)
             dest[rows(p, CAP), C:] = jnp.where(high, value, 0.0).astype(BF16)
             return carry
 
-        lax.fori_loop(0, count, turn, 0)
-
-    def solve(step):
+        lax.fori_loop(begin, begin + N, turn, 0)
+
+    def inflow(begin):
+        for first in range(0, NODES, BLK):
+            part = slice(first, first + BLK)
+            slots = slice(begin * CAP, (begin + N) * CAP)
+            came = jnp.dot(gt_op[part, slots], f2[slots, :], preferred_element_type=F32)
+            for a in range(2):
+                total = acc[a, part, :] + came[:, a * C : (a + 1) * C]
+                if begin:
+                    acc[a, part, :] = total
+                else:
+                    mixed2[part, a * C : (a + 1) * C] = total.astype(BF16)
+
+    def solve_walls(step):
+        drain(peers_of(recv_f, step), v_recv.at[step])
+        flux_of(wall_rate, recv_f, send_f, f2, step, 0, N)
+        inflow(N)
+
+    def solve_crossing(step):
         drain(peers_of(recv_f, step), x_recv.at[step])
-        drain(peers_of(recv_f, step), v_recv.at[step])
-        flux_of(recv_f, send_f, f2, step, 0, 2 * N)
-
-        inflow = jnp.dot(gt_op[...], f2[...], preferred_element_type=F32)
-        for a in range(2):
-            mixed2[:, a * C : (a + 1) * C] = (
-                acc[a] + inflow[:, a * C : (a + 1) * C]
-            ).astype(BF16)
+        flux_of(cross_rate, recv_f, send_f, f2, step, 0, 0)
+        inflow(0)
 
     def advance():
         loads[3].wait()
         for a in range(2):
-            conc2[:, a * C : (a + 1) * C] = solved_half(inv_v, mixed2, len_s, a)
+            for first in range(0, NODES, BLK):
+                conc2[first : first + BLK, a * C : (a + 1) * C] = solved_rows(
+                    inv_v, mixed2, lens, a, first, BLK
+                )
 
     comp_rate = comp_v[...]
     cap = cap_v[...]
     aff = aff_v[...]
 
-    def diffuse(step):
-        drain(peers_of(recv_w, step), w_recv.at[step])
-        flux_of(recv_w, send_r, fr2, step, 2 * N, N)
-        gain[...] = jnp.dot(rt_op[...], fr2[...], preferred_element_type=F32)
+    def stencil(step):
         drain(edge_in.at[step], h_recv.at[step])
         w_ref[step, 0, 8 : 8 + TY, :] = jnp.where(first_r, 0.0, edge_in[step, 0, :TY, :].astype(F32))
         w_ref[step, TX + 1, 8 : 8 + TY, :] = jnp.where(last_r, 0.0, edge_in[step, 1, :TY, :].astype(F32))
@@ -431,33 +449,54 @@
             w_ref[step, x + 1, 7:8, :] = yh[0, x : x + 1, :]
             w_ref[step, x + 1, 8 + TY : 9 + TY, :] = yh[1, x : x + 1, :]
         for x in range(TX):
-            half, low = divmod(x, 8)
             old = r_ref[x]
             around = (w_ref[step, x, 8 : 8 + TY, :] + w_ref[step, x + 2, 8 : 8 + TY, :]) + (
                 w_ref[step, x + 1, 7 : 7 + TY, :] + w_ref[step, x + 1, 9 : 9 + TY, :]
             )
             diffusion = comp_rate * (s_bc[x] * around - t_bc[x] * old)
-            added = diffusion + gain[low * TY : (low + 1) * TY, half * C : (half + 1) * C]
             root = 1.0 + aff * jnp.abs(old)
             square = root * root
-            new = old + added * square / (square + cap)
-            if step == STEPS - 1:
-                rock_o[:, x, :] = jnp.transpose(new)
-            else:
-                _, _, small = put_state(step + 1, x, new)
-                rock2[low * TY : (low + 1) * TY, half * C : (half + 1) * C] = small
-
-    solve(0)
+            share = square / (square + cap)
+            r_ref[x] = old + diffusion * share
+            fac[x] = share
+
+    def absorb(step):
+        drain(peers_of(recv_w, step), w_recv.at[step])
+        flux_of(wall_rate, recv_w, send_r, fr2, step, 2 * N, 0)
+        for low in range(0, 8, 2):
+            gain = jnp.dot(
+                rt_op[low * TY : (low + 2) * TY, :], fr2[...], preferred_element_type=F32
+            )
+            for half in range(2):
+                for i in range(2):
+                    x = half * 8 + low + i
+                    new = r_ref[x] + fac[x] * gain[
+                        i * TY : (i + 1) * TY, half * C : (half + 1) * C
+                    ]
+                    if step == STEPS - 1:
+                        rock_o[:, x, :] = jnp.transpose(new)
+                    else:
+                        put_state(step + 1, x, new)
+
+    stencil(0)
+    absorb(0)
+    edges(1)
+    for copy in halo_copies(1):
+        copy.start()
+    gather(r_op, rock2, 2 * N * CAP, send_r, 1, 0)
+    send_rock(1)
+    solve_walls(0)
+    solve_crossing(0)
     advance()
-    gather(g_op, conc2, 0, send_f, 1)
-    send_fractures(1)
-    diffuse(0)
-    edges(1)
-    gather(r_op, rock2, 2 * N * CAP, send_r, 1)
-    send_rock(1)
+    gather(g_op, conc2, 0, send_f, 1, 0)
+    send_crossing(1)
+    gather(g_op, conc2, 0, send_f, 1, 1)
+    send_walls(1)
     product()
-    diffuse(1)
-    solve(1)
+    stencil(1)
+    solve_walls(1)
+    absorb(1)
+    solve_crossing(1)
 
     drain(dh, d_send)
     for step in range(STEPS):
@@ -467,20 +506,20 @@
         drain(edge_out.at[step], h_send.at[step])
 
 
-def finish(len_h, inv_v, mixed2, rock_v, conc_h, rock_h, len_s, conc_v, sem):
-    rock_copy = pltpu.make_async_copy(rock_v, rock_h, sem.at[2])
+def finish(inv_v, mixed2, rock_v, lens, conc_h, rock_h, conc_v, sem):
+    rock_copy = pltpu.make_async_copy(rock_v, rock_h, sem.at[0])
     rock_copy.start()
-    len_copy = pltpu.make_async_copy(len_h, len_s, sem.at[3])
-    len_copy.start()
-    len_copy.wait()
-    copies = []
+    copies = [rock_copy]
     for a in range(2):
-        conc_v[a] = solved_half(inv_v, mixed2, len_s, a)
-        copies.append(pltpu.make_async_copy(conc_v.at[a], conc_h.at[a], sem.at[a]))
-        copies[-1].start()
+        for first in range(0, NODES, BLK):
+            part = (a, pl.ds(first, BLK))
+            conc_v[a, first : first + BLK, :] = solved_rows(inv_v, mixed2, lens, a, first, BLK)
+            copies.append(
+                pltpu.make_async_copy(conc_v.at[part], conc_h.at[part], sem.at[len(copies)])
+            )
+            copies[-1].start()
     for copy in copies:
         copy.wait()
-    rock_copy.wait()
 
 
 def local(
@@ -506,15 +545,16 @@
     def stay(x):
         return pltpu.with_memory_space_constraint(x, pltpu.HBM)
 
-    inverse, mixed, rock = pl.pallas_call(
+    inverse, mixed, rock, lens = pl.pallas_call(
         kernel,
         out_shape=(
             V(frac_inverse.shape, BF16),
             V((NODES, 2 * C), BF16),
             V(rock_conc.shape, F32),
+            V((8, C), jnp.int32),
         ),
         in_specs=[any_spec] * 14,
-        out_specs=(vmem, vmem, vmem),
+        out_specs=(vmem, vmem, vmem, vmem),
         scratch_shapes=[
             pltpu.SMEM((2,), jnp.int32),
             V((N, CAP), jnp.int32),
@@ -549,7 +589,7 @@
             V((TX, TY, C), F32),
             V((TX, TY, C), F32),
             V((STEPS, TX + 2, TY + 16, C), F32),
-            V((NODES, 2 * C), F32),
+            V((TX, TY, C), F32),
             V((4, TX, TY), F32),
             V((2, TX, C), F32),
             V((2, TX, C), F32),
@@ -593,12 +633,12 @@
             jax.ShapeDtypeStruct(frac_conc.shape, BF16),
             jax.ShapeDtypeStruct(rock_conc.shape, F32),
         ),
-        in_specs=[any_spec, vmem, vmem, vmem],
+        in_specs=[vmem, vmem, vmem, vmem],
         out_specs=(any_spec, any_spec),
-        scratch_shapes=[pltpu.SMEM((2,), jnp.int32), V(frac_conc.shape, BF16), dma((4,))],
+        scratch_shapes=[V(frac_conc.shape, BF16), dma((1 + 2 * NODES // BLK,))],
         compiler_params=pltpu.CompilerParams(vmem_limit_bytes=8 << 20),
         name="finish",
-    )(stay(frac_len), inverse, mixed, rock)
+    )(inverse, mixed, rock, lens)
 
 
 def solution(mesh):

time: 36.7 us -> 32.4 us (0.88)
  Pallas kernels: 35.9 us -> 31.6 us
    pallas_call x1, Pallas kernels: 33.2 us -> 29.7 us  [local(): pl.pallas_call(kernel, out_shape=(V(frac_inverse.shape, BF16), V((NODES,...]
    pallas_call x1, Pallas kernels: 2.73 us -> 1.96 us  [local(): pl.pallas_call(finish, out_shape=(jax.ShapeDtypeStruct(frac_conc.shape, B...]
where the time goes in v3:
time: 32.4 us; the launch traced here: 32.3 us
  Pallas kernels  31.6 us (98%)
  between operations  0.64 us (2%)
    pallas_call x1, Pallas kernels, local(): pl.pallas_call(kernel, out_shape=(V(frac_inverse.shape, BF16), V((NODES,...  29.7 us
    pallas_call x1, Pallas kernels, local(): pl.pallas_call(finish, out_shape=(jax.ShapeDtypeStruct(frac_conc.shape, B...  1.96 us

profile of v3, /device:TPU:1, one launch (start us, length us, event | category | flops | bytes accessed | tf_op | source)
XLA Modules:
  0.0 32.3 jit_solution(5713175768346697652)
XLA Ops:
  0.6 29.7 %tracer_steps.1 = (bf16[2,1024,1024]{2,1,0:T(8,128)(2,1)S(1)}, bf16[1024,256]{1,0:T(8,128)(2,1)S(1)}, f32[128,16,128]{2,1,0:T(8,128)S(1)}, s32[8,128]{1,0:T(8,128)S(1)}) custom-call(bf16[2,1024,128]{2,1,0:T(8,128)(2,1)} %conc_h.1, s32[2]{0:T(128)} %len_h.1, bf16[2,1024,1024]{2,1,0:T(8,128)(2,1)} %flux_h.1, bf16[2,1024,1024]{2,1,0:T(8,128)(2,1)} %inv_h.1, ...), custom_call_target="tpu_custom_call" | custom-call | tf_op jit(solution)/shard_map/tracer_steps/pallas_call | solution.py:548
  30.3 2.0 %finish.1 = (bf16[2,1024,128]{2,1,0:T(8,128)(2,1)}, f32[128,16,128]{2,1,0:T(8,128)}) custom-call(bf16[2,1024,1024]{2,1,0:T(8,128)(2,1)S(1)} %get-tuple-element.6.inv_v, bf16[1024,256]{1,0:T(8,128)(2,1)S(1)} %get-tuple-element.7.mixed2, f32[128,16,128]{2,1,0:T(8,128)S(1)} %get-tuple-element.8.rock_v, s32[8,128]{1,0:T(8,128)S(1)} %get-tuple-element.9.lens), custom_call_target="tpu_custom_call" | custom-call | tf_op jit(solution)/shard_map/finish/pallas_call | solution.py:630

commit v4 on v3

--- a/solution.py
+++ b/solution.py
@@ -43,6 +43,15 @@
     )
     node = lax.broadcasted_iota(jnp.int32, (count, C), 0) + first
     return jnp.where(node < lens[a : a + 1, :], solved, 0.0).astype(BF16)
+
+
+def absorbed(rt_op, fr2, r_ref, fac, low):
+    gain = jnp.dot(rt_op[low * TY : (low + 2) * TY, :], fr2[...], preferred_element_type=F32)
+    for half in range(2):
+        for i in range(2):
+            x = half * 8 + low + i
+            brought = gain[i * TY : (i + 1) * TY, half * C : (half + 1) * C]
+            yield x, r_ref[x] + fac[x] * brought
 
 
 def kernel(
@@ -62,8 +71,11 @@
     aff_h,
     inv_v,
     mixed2,
-    rock_o,
     lens,
+    r_ref,
+    fac,
+    fr2,
+    rt_op,
     len_s,
     inter_v,
     wall_v,
@@ -85,19 +97,15 @@
     g_op,
     gt_op,
     r_op,
-    rt_op,
     f2,
-    fr2,
     send_f,
     recv_f,
     send_r,
     recv_w,
-    r_ref,
     rock2,
     s_bc,
     t_bc,
     w_ref,
-    fac,
     dh,
     ye,
     yh,
@@ -347,8 +355,6 @@
     table[2 * N : 3 * N, 0:CAP] = cells_v[...].astype(F32)
     spread_slots(2 * N, 3 * N)
     build_gather(r_op, 8, 4)
-    gather(r_op, rock2, 2 * N * CAP, send_r, 0, 0)
-    send_rock(0)
 
     for j in range(12):
         row = jnp.zeros((8, 128), F32)
@@ -370,6 +376,8 @@
 
     loads[2].wait()
     product()
+    gather(r_op, rock2, 2 * N * CAP, send_r, 0, 0)
+    send_rock(0)
 
     drain(dh, d_recv)
     xrow = lax.broadcasted_iota(jnp.int32, (TX, TY), 0)
@@ -405,27 +413,27 @@
 
         lax.fori_loop(begin, begin + N, turn, 0)
 
-    def inflow(begin):
+    def inflow(begin, last):
         for first in range(0, NODES, BLK):
             part = slice(first, first + BLK)
             slots = slice(begin * CAP, (begin + N) * CAP)
             came = jnp.dot(gt_op[part, slots], f2[slots, :], preferred_element_type=F32)
             for a in range(2):
                 total = acc[a, part, :] + came[:, a * C : (a + 1) * C]
-                if begin:
+                if last:
+                    mixed2[part, a * C : (a + 1) * C] = total.astype(BF16)
+                else:
                     acc[a, part, :] = total
-                else:
-                    mixed2[part, a * C : (a + 1) * C] = total.astype(BF16)
-
-    def solve_walls(step):
+
+    def solve_walls(step, last):
         drain(peers_of(recv_f, step), v_recv.at[step])
         flux_of(wall_rate, recv_f, send_f, f2, step, 0, N)
-        inflow(N)
-
-    def solve_crossing(step):
+        inflow(N, last)
+
+    def solve_crossing(step, last):
         drain(peers_of(recv_f, step), x_recv.at[step])
         flux_of(cross_rate, recv_f, send_f, f2, step, 0, 0)
-        inflow(0)
+        inflow(0, last)
 
     def advance():
         loads[3].wait()
@@ -463,20 +471,10 @@
     def absorb(step):
         drain(peers_of(recv_w, step), w_recv.at[step])
         flux_of(wall_rate, recv_w, send_r, fr2, step, 2 * N, 0)
-        for low in range(0, 8, 2):
-            gain = jnp.dot(
-                rt_op[low * TY : (low + 2) * TY, :], fr2[...], preferred_element_type=F32
-            )
-            for half in range(2):
-                for i in range(2):
-                    x = half * 8 + low + i
-                    new = r_ref[x] + fac[x] * gain[
-                        i * TY : (i + 1) * TY, half * C : (half + 1) * C
-                    ]
-                    if step == STEPS - 1:
-                        rock_o[:, x, :] = jnp.transpose(new)
-                    else:
-                        put_state(step + 1, x, new)
+        if step < STEPS - 1:
+            for low in range(0, 8, 2):
+                for x, new in absorbed(rt_op, fr2, r_ref, fac, low):
+                    put_state(step + 1, x, new)
 
     stencil(0)
     absorb(0)
@@ -485,8 +483,8 @@
         copy.start()
     gather(r_op, rock2, 2 * N * CAP, send_r, 1, 0)
     send_rock(1)
-    solve_walls(0)
-    solve_crossing(0)
+    solve_crossing(0, False)
+    solve_walls(0, True)
     advance()
     gather(g_op, conc2, 0, send_f, 1, 0)
     send_crossing(1)
@@ -494,9 +492,9 @@
     send_walls(1)
     product()
     stencil(1)
-    solve_walls(1)
+    solve_walls(1, False)
     absorb(1)
-    solve_crossing(1)
+    solve_crossing(1, True)
 
     drain(dh, d_send)
     for step in range(STEPS):
@@ -506,18 +504,29 @@
         drain(edge_out.at[step], h_send.at[step])
 
 
-def finish(inv_v, mixed2, rock_v, lens, conc_h, rock_h, conc_v, sem):
-    rock_copy = pltpu.make_async_copy(rock_v, rock_h, sem.at[0])
-    rock_copy.start()
-    copies = [rock_copy]
-    for a in range(2):
-        for first in range(0, NODES, BLK):
-            part = (a, pl.ds(first, BLK))
-            conc_v[a, first : first + BLK, :] = solved_rows(inv_v, mixed2, lens, a, first, BLK)
-            copies.append(
-                pltpu.make_async_copy(conc_v.at[part], conc_h.at[part], sem.at[len(copies)])
-            )
-            copies[-1].start()
+def finish(
+    inv_v, mixed2, lens, r_ref, fac, fr2, rt_op, conc_h, rock_h, conc_v, rock_v, sem
+):
+    def solve_part(a, first):
+        conc_v[a, first : first + BLK, :] = solved_rows(inv_v, mixed2, lens, a, first, BLK)
+
+    for low in range(0, 8, 2):
+        for x, new in absorbed(rt_op, fr2, r_ref, fac, low):
+            rock_v[:, x, :] = jnp.transpose(new)
+        solve_part(0, low // 2 * BLK)
+    copies = [
+        pltpu.make_async_copy(rock_v, rock_h, sem.at[0]),
+        pltpu.make_async_copy(conc_v.at[0], conc_h.at[0], sem.at[1]),
+    ]
+    copies[0].start()
+    copies[1].start()
+    for first in range(0, NODES, BLK):
+        solve_part(1, first)
+        part = (1, pl.ds(first, BLK))
+        copies.append(
+            pltpu.make_async_copy(conc_v.at[part], conc_h.at[part], sem.at[len(copies)])
+        )
+        copies[-1].start()
     for copy in copies:
         copy.wait()
 
@@ -545,16 +554,19 @@
     def stay(x):
         return pltpu.with_memory_space_constraint(x, pltpu.HBM)
 
-    inverse, mixed, rock, lens = pl.pallas_call(
+    passed = pl.pallas_call(
         kernel,
         out_shape=(
             V(frac_inverse.shape, BF16),
             V((NODES, 2 * C), BF16),
-            V(rock_conc.shape, F32),
             V((8, C), jnp.int32),
+            V((TX, TY, C), F32),
+            V((TX, TY, C), F32),
+            V((N * CAP, 2 * C), BF16),
+            V((NODES, N * CAP), BF16),
         ),
         in_specs=[any_spec] * 14,
-        out_specs=(vmem, vmem, vmem, vmem),
+        out_specs=(vmem,) * 7,
         scratch_shapes=[
             pltpu.SMEM((2,), jnp.int32),
             V((N, CAP), jnp.int32),
@@ -577,19 +589,15 @@
             V((2 * N * CAP, NODES), BF16),
             V((NODES, 2 * N * CAP), BF16),
             V((N * CAP, NODES), BF16),
-            V((NODES, N * CAP), BF16),
             V((2 * N * CAP, 2 * C), BF16),
-            V((N * CAP, 2 * C), BF16),
             V((STEPS, 2 * N, CAP, C), BF16),
             V((STEPS, 2 * N, CAP, C), BF16),
             V((STEPS, N, CAP, C), BF16),
             V((STEPS, N, CAP, C), BF16),
-            V((TX, TY, C), F32),
             V((NODES, 2 * C), BF16),
             V((TX, TY, C), F32),
             V((TX, TY, C), F32),
             V((STEPS, TX + 2, TY + 16, C), F32),
-            V((TX, TY, C), F32),
             V((4, TX, TY), F32),
             V((2, TX, C), F32),
             V((2, TX, C), F32),
@@ -633,12 +641,12 @@
             jax.ShapeDtypeStruct(frac_conc.shape, BF16),
             jax.ShapeDtypeStruct(rock_conc.shape, F32),
         ),
-        in_specs=[vmem, vmem, vmem, vmem],
+        in_specs=[vmem] * 7,
         out_specs=(any_spec, any_spec),
-        scratch_shapes=[V(frac_conc.shape, BF16), dma((1 + 2 * NODES // BLK,))],
+        scratch_shapes=[V(frac_conc.shape, BF16), V(rock_conc.shape, F32), dma((2 + NODES // BLK,))],
         compiler_params=pltpu.CompilerParams(vmem_limit_bytes=8 << 20),
         name="finish",
-    )(inverse, mixed, rock, lens)
+    )(*passed)
 
 
 def solution(mesh):

time: 32.4 us -> 31 us (0.957)
  Pallas kernels: 31.6 us -> 30.2 us
    pallas_call x1, Pallas kernels: 29.7 us -> 27.6 us  [local(): pl.pallas_call(kernel, out_shape=(V(frac_inverse.shape, BF16), V((NODES,...]
    pallas_call x1, Pallas kernels: 1.96 us -> 2.58 us  [local(): pl.pallas_call(finish, out_shape=(jax.ShapeDtypeStruct(frac_conc.shape, B...]
where the time goes in v4:
time: 31 us; the launch traced here: 30.8 us
  Pallas kernels  30.2 us (97%)
  between operations  0.64 us (2%)
    pallas_call x1, Pallas kernels, local(): pl.pallas_call(kernel, out_shape=(V(frac_inverse.shape, BF16), V((NODES,...  27.6 us
    pallas_call x1, Pallas kernels, local(): pl.pallas_call(finish, out_shape=(jax.ShapeDtypeStruct(frac_conc.shape, B...  2.58 us

profile of v4, /device:TPU:1, one launch (start us, length us, event | category | flops | bytes accessed | tf_op | source)
XLA Modules:
  0.0 30.8 jit_solution(2307926032879798088)
XLA Ops:
  0.6 27.6 %tracer_steps.1 = (bf16[2,1024,1024]{2,1,0:T(8,128)(2,1)S(1)}, bf16[1024,256]{1,0:T(8,128)(2,1)S(1)}, s32[8,128]{1,0:T(8,128)S(1)}, f32[16,128,128]{2,1,0:T(8,12...) custom-call(bf16[2,1024,128]{2,1,0:T(8,128)(2,1)} %conc_h.1, ...), custom_call_target="tpu_custom_call" | custom-call | tf_op jit(solution)/shard_map/tracer_steps/pallas_call | solution.py:557
  28.2 2.6 %finish.1 = (bf16[2,1024,128]{2,1,0:T(8,128)(2,1)}, f32[128,16,128]{2,1,0:T(8,128)}) custom-call(bf16[2,1024,1024]{2,1,0:T(8,128)(2,1)S(1)} %get-tuple-element.9.inv_v, bf16[1024,256]{1,0:T(8,128)(2,1)S(1)} %get-tuple-element.10.mixed2, s32[8,128]{1,0:T(8,128)S(1)} %get-tuple-element.11.lens, f32[16,128,128]{2,1,0:T(8,128)S(1)} %get-tuple-element.12.r_ref, ...), custom_call_target="tpu_custom_call" | custom-call | tf_op jit(solution)/shard_map/finish/pallas_call | solution.py:638

commit v5 on v4

--- a/solution.py
+++ b/solution.py
@@ -208,17 +208,20 @@
     )
 
     def diff_copies():
-        return [
-            pltpu.make_async_remote_copy(
-                src_ref=diff_v,
-                dst_ref=dh.at[side],
-                send_sem=d_send,
-                recv_sem=d_recv,
-                device_id=device,
-                device_id_type=MESH,
+        out = []
+        for device, side in sides:
+            part = (pl.ds(TX - 8, 8), pl.ds(0, 8), pl.ds(0, TX), pl.ds(0, TX))[side]
+            out.append(
+                pltpu.make_async_remote_copy(
+                    src_ref=diff_v.at[part],
+                    dst_ref=dh.at[side, part],
+                    send_sem=d_send,
+                    recv_sem=d_recv,
+                    device_id=device,
+                    device_id_type=MESH,
+                )
             )
-            for device, side in sides
-        ]
+        return out
 
     def halo_copies(step):
         out = []
@@ -379,16 +382,15 @@
     gather(r_op, rock2, 2 * N * CAP, send_r, 0, 0)
     send_rock(0)
 
-    drain(dh, d_recv)
+    drain(dh.at[pl.ds(0, 3)], d_recv)
     xrow = lax.broadcasted_iota(jnp.int32, (TX, TY), 0)
     ycol = lax.broadcasted_iota(jnp.int32, (TX, TY), 1)
-    side_s = jnp.sqrt(dh[...])
     first_r, last_r = me_r == 0, me_r == N - 1
     first_f, last_f = me_f == 0, me_f == N - 1
-    down_x = jnp.where(first_r, 0.0, side_s[0, TX - 1 :, :])
-    up_x = jnp.where(last_r, 0.0, side_s[1, :1, :])
-    down_y = jnp.where(first_f, 0.0, pltpu.roll(side_s[2], 1, 1))
-    up_y = jnp.where(last_f, 0.0, pltpu.roll(side_s[3], TY - 1, 1))
+    down_x = jnp.where(first_r, 0.0, jnp.sqrt(dh[0, TX - 1 :, :]))
+    up_x = jnp.where(last_r, 0.0, jnp.sqrt(dh[1, :1, :]))
+    down_y = jnp.where(first_f, 0.0, pltpu.roll(jnp.sqrt(dh[2]), 1, 1))
+    up_y = jnp.where(last_f, 0.0, pltpu.roll(jnp.sqrt(dh[3]), TY - 1, 1))
     total = jnp.where(xrow == 0, down_x, pltpu.roll(s_here, 1, 0))
     total = total + jnp.where(xrow == TX - 1, up_x, pltpu.roll(s_here, TX - 1, 0))
     total = total + jnp.where(ycol == 0, down_y, pltpu.roll(s_here, 1, 1))
@@ -404,14 +406,16 @@
     wall_rate = wrate_v[...]
 
     def flux_of(rate, recv, send, dest, step, first, begin):
-        def turn(p, carry):
-            value = rate * (recv[step, p].astype(F32) - send[step, p].astype(F32))
-            high = idxb[rows(first + p, CAP), :] >= NODES
-            dest[rows(p, CAP), :C] = jnp.where(high, 0.0, value).astype(BF16)
-            dest[rows(p, CAP), C:] = jnp.where(high, value, 0.0).astype(BF16)
-            return carry
-
-        lax.fori_loop(begin, begin + N, turn, 0)
+        for p in range(begin, begin + N, 4):
+            part = slice(p * CAP, (p + 4) * CAP)
+            here = slice((first + p) * CAP, (first + p + 4) * CAP)
+            value = rate * (
+                recv[step, p : p + 4].reshape(4 * CAP, C).astype(F32)
+                - send[step, p : p + 4].reshape(4 * CAP, C).astype(F32)
+            )
+            high = idxb[here, :] >= NODES
+            dest[part, :C] = jnp.where(high, 0.0, value).astype(BF16)
+            dest[part, C:] = jnp.where(high, value, 0.0).astype(BF16)
 
     def inflow(begin, last):
         for first in range(0, NODES, BLK):
@@ -496,7 +500,7 @@
     absorb(1)
     solve_crossing(1, True)
 
-    drain(dh, d_send)
+    drain(dh.at[pl.ds(0, 3)], d_send)
     for step in range(STEPS):
         drain(peers_of(send_f, step), x_send.at[step])
         drain(peers_of(send_f, step), w_send.at[step])

time: 31 us -> 30.6 us (0.987)
  Pallas kernels: 30.2 us -> 29.6 us
    pallas_call x1, Pallas kernels: 27.6 us -> 27 us  [local(): pl.pallas_call(kernel, out_shape=(V(frac_inverse.shape, BF16), V((NODES,...]
where the time goes in v5:
time: 30.6 us; the launch traced here: 30.4 us
  Pallas kernels  29.6 us (97%)
  between operations  0.8 us (3%)
    pallas_call x1, Pallas kernels, local(): pl.pallas_call(kernel, out_shape=(V(frac_inverse.shape, BF16), V((NODES,...  27 us
    pallas_call x1, Pallas kernels, local(): pl.pallas_call(finish, out_shape=(jax.ShapeDtypeStruct(frac_conc.shape, B...  2.58 us

profile of v5, /device:TPU:1, one launch (start us, length us, event | category | flops | bytes accessed | tf_op | source)
XLA Modules:
  0.0 30.4 jit_solution(15533638092976318186)
XLA Ops:
  0.6 27.0 %tracer_steps.1 = (bf16[2,1024,1024]{2,1,0:T(8,128)(2,1)S(1)}, bf16[1024,256]{1,0:T(8,128)(2,1)S(1)}, s32[8,128]{1,0:T(8,128)S(1)}, f32[16,128,128]{2,1,0:T(8,12...) custom-call(bf16[2,1024,128]{2,1,0:T(8,128)(2,1)} %conc_h.1, ...), custom_call_target="tpu_custom_call" | custom-call | tf_op jit(solution)/shard_map/tracer_steps/pallas_call | solution.py:561
  27.7 2.6 %finish.1 = (bf16[2,1024,128]{2,1,0:T(8,128)(2,1)}, f32[128,16,128]{2,1,0:T(8,128)}) custom-call(bf16[2,1024,1024]{2,1,0:T(8,128)(2,1)S(1)} %get-tuple-element.9.inv_v, bf16[1024,256]{1,0:T(8,128)(2,1)S(1)} %get-tuple-element.10.mixed2, s32[8,128]{1,0:T(8,128)S(1)} %get-tuple-element.11.lens, f32[16,128,128]{2,1,0:T(8,128)S(1)} %get-tuple-element.12.r_ref, ...), custom_call_target="tpu_custom_call" | custom-call | tf_op jit(solution)/shard_map/finish/pallas_call | solution.py:642
